TPU v7x, 32 devices: a whole 2x2x4 slice. The times are simulated.
32 devices in a mesh: gx: 8 (over z, core), gy: 4 (over y, x).
Axes of the slice: x: 2, y: 2, z: 4, core: 2. Of those that a mesh axis runs over, the one named last changes fastest.
Arguments:
- raw_stack: float32 [2, 32, 128, 2048], P(None, ('gx', 'gy')), may hold values from 0 to 8
- psf_taps: float32 [3, 2, 31], replicated, may hold values from 0.05 to 1
Outputs:
- estimate: float32 [2, 32, 128, 2048], P(None, None, 'gy', 'gx')
All inputs are finite; a program needn't handle non-finite values.
Results may differ from a plain program's by a relative error of at most 0.0001.
Values sent between devices are 32-bit elements; how exact they have to be, the bound alone decides.
A program may use at most 192 MiB of HBM per device.

v0:
```python
import jax
import jax.numpy as jnp
from jax import lax
from jax.sharding import PartitionSpec as P

ITERS = 2


BACKGROUND = 0.5
SIGMA_ACROSS = 48.0
SIGMA_ALONG = 96.0


def padded(block, sides, width):
    for axis, dim in sides:
        count = lax.axis_size(axis)
        forward = [(i, i + 1) for i in range(count - 1)]
        backward = [(target, source) for source, target in forward]
        low = lax.ppermute(
            lax.slice_in_dim(block, block.shape[dim] - width, None, axis=dim), axis, forward
        )
        high = lax.ppermute(lax.slice_in_dim(block, 0, width, axis=dim), axis, backward)
        block = jnp.concatenate([low, block, high], axis=dim)
    return block


def smoothing_table(length_cells, spread_cells, circular):
    places = lax.iota(jnp.int32, length_cells)
    offset = jnp.abs(places[:, None] - places[None, :])
    if circular:
        offset = jnp.minimum(offset, length_cells - offset)
    scaled = offset.astype(jnp.float32) / spread_cells
    kernel_table = jnp.exp(-0.5 * scaled * scaled)
    return kernel_table / jnp.sum(kernel_table, axis=1, keepdims=True)


def band_matrix(kernel_taps, size_in, size_out, start_lag):
    rows_in = lax.iota(jnp.int32, size_in)
    rows_out = lax.iota(jnp.int32, size_out)
    tap_index = lax.iota(jnp.int32, kernel_taps.shape[1])
    lag_grid = rows_in[:, None] - rows_out[None, :] - start_lag
    onehot = (lag_grid[:, :, None] == tap_index[None, None, :]).astype(jnp.float32)
    return jnp.einsum("jik,ck->cji", onehot, kernel_taps, precision=lax.Precision.HIGHEST)


def along_depth(volume, matrix):
    return jnp.einsum("cjxy,cji->cixy", volume, matrix, precision=lax.Precision.HIGHEST)


def along_rows(volume, matrix):
    return jnp.einsum("czjy,cji->cziy", volume, matrix, precision=lax.Precision.HIGHEST)


def along_lines(volume, matrix):
    return jnp.einsum("czxj,cji->czxi", volume, matrix, precision=lax.Precision.HIGHEST)


def blur_local(volume, kernel_set, half_taps):
    planes_count = volume.shape[1]
    filtered = along_depth(
        volume, band_matrix(kernel_set[0], planes_count, planes_count, -half_taps)
    )
    widened = padded(filtered, (("gy", 2),), half_taps)
    filtered = along_rows(
        widened, band_matrix(kernel_set[1], widened.shape[2], filtered.shape[2], 0)
    )
    widened = padded(filtered, (("gx", 3),), half_taps)
    return along_lines(widened, band_matrix(kernel_set[2], widened.shape[3], filtered.shape[3], 0))


def local(raw_stack, psf_taps):
    half_taps = psf_taps.shape[2] // 2
    channels = raw_stack.shape[0]
    lines_x = raw_stack.shape[2]
    lines_y = raw_stack.shape[3]
    count_gx = lax.axis_size("gx")
    count_gy = lax.axis_size("gy")
    width_x = lines_x // count_gy
    width_y = lines_y // count_gx
    across_table = smoothing_table(lines_x, SIGMA_ACROSS, False)
    along_table = smoothing_table(lines_y, SIGMA_ALONG, True)
    smoothed = jnp.einsum("ij,czjy->cziy", across_table, raw_stack, precision=lax.Precision.HIGHEST)
    stripes = smoothed - jnp.einsum(
        "czxj,jy->czxy", smoothed, along_table, precision=lax.Precision.HIGHEST
    )
    cleaned_plane = jnp.maximum(raw_stack - stripes, 0.0)
    blocks = cleaned_plane.reshape(channels, count_gy, width_x, count_gx, width_y)
    blocks = jnp.transpose(blocks, (3, 1, 0, 2, 4)).reshape(
        count_gx * count_gy, channels, 1, width_x, width_y
    )
    regrouped = lax.all_to_all(blocks, ("gx", "gy"), split_axis=0, concat_axis=2, tiled=True)
    cleaned = regrouped.reshape(channels, count_gx * count_gy, width_x, width_y)
    forward = psf_taps / jnp.sum(psf_taps, axis=2, keepdims=True)
    backward = forward[:, :, ::-1]
    estimate = cleaned
    for iteration in range(ITERS):
        blurred = blur_local(estimate, forward, half_taps)
        ratio_field = cleaned / (blurred + BACKGROUND)
        estimate = estimate * blur_local(ratio_field, backward, half_taps)
    return estimate


def solution(mesh):
    in_specs = (P(None, ("gx", "gy"), None, None), P())
    out_specs = P(None, None, "gy", "gx")
    return jax.shard_map(local, mesh=mesh, in_specs=in_specs, out_specs=out_specs, check_vma=False)
```

profile of v0, /device:TPU:1, one launch (start us, length us, event | category | flops | bytes accessed | tf_op | source)
XLA Modules:
  0.0 430.6 jit_solution(16689278205702244576)
XLA Ops:
  0.1 8.0 %fusion.4 = f32[2048]{0:T(1024)S(1)} fusion(), kind=kLoop, calls=%fused_computation.6 | loop fusion | flops 37746688 | bytes 8192 | tf_op jit(solution)/shard_map/reduce_sum | solution.py:34
  10.1 23.3 %fusion.38 = f32[2,1,128,2048]{3,2,0,1:T(8,128)S(1)} fusion(f32[2048]{0:T(1024)S(1)} %fusion.4, f32[128,2,2048]{2,0,1:T(8,128)S(1)} %fusion.46, f32[2,1,128,2048]{3,2,1,0:T(8,128)S(1)} %copy-done.11), kind=kOutput, calls=%fused_computation.43 | convolution fusion | flops 12924223488 | bytes 6299648 | tf_op jit(solution)/shard_map/czxj,jy->czxy/dot_general | solution.py:83
  36.2 7.1 %all-to-all-start = ((f32[32,2,1,32,256]{4,3,1,2,0:T(8,128)}), f32[32,2,1,32,256]{4,3,1,2,0:T(8,128)S(1)}, u32[]{:S(2)}, u32[]{:S(2)}) async-start(f32[32,2,1,32,256]{4,3,1,2,0:T(8,128)} %bitcast.112), calls=%async_computation | async-start | bytes 4194304 | tf_op jit(solution)/shard_map/all_to_all | solution.py:91
  44.8 46.5 %all-to-all-done = f32[32,2,1,32,256]{4,3,1,2,0:T(8,128)S(1)} async-done(((f32[32,2,1,32,256]{4,3,1,2,0:T(8,128)}), f32[32,2,1,32,256]{4,3,1,2,0:T(8,128)S(1)}, u32[]{:S(2)}, u32[]{:S(2)}) %all-to-all-start) | async-done | bytes 2097184 | tf_op jit(solution)/shard_map/all_to_all | solution.py:91
  95.9 3.2 collective-permute-start
  102.8 16.8 %collective-permute-done = f32[2,32,15,256]{3,1,2,0:T(8,128)S(1)} collective-permute-done((f32[2,32,15,256]{3,1,2,0:T(8,128)}, f32[2,32,15,256]{3,1,2,0:T(8,128)S(1)}, u32[]{:S(2)}, u32[]{:S(2)}) %collective-permute-start) | collective-permute-done | bytes 983072 | tf_op jit(solution)/shard_map/ppermute | solution.py:19
  119.6 23.6 %collective-permute-done.1 = f32[2,32,15,256]{3,1,2,0:T(8,128)S(1)} collective-permute-done((f32[2,32,15,256]{3,1,2,0:T(8,128)S(1)}, f32[2,32,15,256]{3,1,2,0:T(8,128)S(1)}, u32[]{:S(2)}, u32[]{:S(2)}) %collective-permute-start.1) | collective-permute-done | bytes 983072 | tf_op jit(solution)/shard_map/ppermute | solution.py:22
  145.2 4.5 %fusion.58 = f32[2,32,32,256]{3,2,1,0:T(8,128)S(1)} fusion(f32[2,32,62,256]{3,1,2,0:T(8,128)S(1)} %pad_maximum_fusion, f32[2,62,32,1]{1,0,2,3:T(2,128)S(1)} %convolution_bitcast_fusion.1), kind=kOutput, calls=%fused_computation.60 | convolution fusion | flops 390070272 | bytes 6176256 | tf_op jit(solution)/shard_map/czjy,cji->cziy/dot_general | solution.py:51
  154.9 3.3 collective-permute-start.3
  160.7 4.5 %fusion.70 = f32[2,286,256,1]{2,0,1,3:T(2,128)} fusion(s32[286,256]{1,0:T(8,128)S(1)} %iota_subtract_fusion, f32[3,2,31]{2,1,0:T(2,128)} %copy-done.14), kind=kOutput, calls=%fused_computation.64 | convolution fusion | flops 56742400 | bytes 879616 | tf_op jit(solution)/shard_map/jik,ck->cji/dot_general | solution.py:43
  173.0 5.5 %fusion.27 = f32[2,32,32,256]{3,1,2,0:T(8,128)S(1)} fusion(f32[2,32,32,286]{3,2,1,0:T(8,128)S(1)} %pad_maximum_fusion.4, f32[2,286,256,1]{2,0,1,3:T(2,128)S(1)} %copy-done.7), kind=kOutput, calls=%fused_computation.38 | convolution fusion | flops 1799356416 | bytes 5025792 | tf_op jit(solution)/shard_map/czxj,cji->czxi/dot_general | solution.py:55
  178.5 3.3 fusion.44
  183.0 3.4 collective-permute-start.4
  188.7 18.2 %collective-permute-done.4 = f32[2,32,15,256]{3,1,2,0:T(8,128)} collective-permute-done((f32[2,32,15,256]{3,1,2,0:T(8,128)}, f32[2,32,15,256]{3,1,2,0:T(8,128)}, u32[]{:S(2)}, u32[]{:S(2)}) %collective-permute-start.4) | collective-permute-done | bytes 983072 | tf_op jit(solution)/shard_map/ppermute | solution.py:19
  207.0 22.1 %collective-permute-done.5 = f32[2,32,15,256]{3,1,2,0:T(8,128)} collective-permute-done((f32[2,32,15,256]{3,1,2,0:T(8,128)S(1)}, f32[2,32,15,256]{3,1,2,0:T(8,128)}, u32[]{:S(2)}, u32[]{:S(2)}) %collective-permute-start.5) | collective-permute-done | bytes 983072 | tf_op jit(solution)/shard_map/ppermute | solution.py:22
  231.0 4.5 %fusion.61 = f32[2,32,32,256]{3,2,1,0:T(8,128)S(1)} fusion(f32[2,32,62,256]{3,1,2,0:T(8,128)S(1)} %pad_maximum_fusion.1, f32[2,62,32,1]{1,0,2,3:T(2,128)S(1)} %convolution_bitcast_fusion.3), kind=kOutput, calls=%fused_computation.61 | convolution fusion | flops 390070272 | bytes 6176256 | tf_op jit(solution)/shard_map/czjy,cji->cziy/dot_general | solution.py:51
  243.1 3.6 collective-permute-start.6
  246.8 3.8 fusion.71
  258.9 6.7 %bitcast_multiply_fusion = f32[2,32,32,256]{3,1,2,0:T(8,128)S(1)} fusion(f32[32,2,1,32,256]{4,3,1,2,0:T(8,128)S(1)} %copy-done.2, f32[2,32,32,286]{3,2,1,0:T(8,128)S(1)} %pad_maximum_fusion.5, f32[2,286,256,1]{2,0,1,3:T(2,128)S(1)} %copy-done.9), kind=kOutput, calls=%fused_computation.46 | convolution fusion | flops 1799880704 | bytes 7122944 | tf_op jit(solution)/shard_map/czxj,cji->czxi/dot_general | solution.py:55
  270.5 18.6 %collective-permute-done.8 = f32[2,32,15,256]{3,1,2,0:T(8,128)S(1)} collective-permute-done((f32[2,32,15,256]{3,1,2,0:T(8,128)S(1)}, f32[2,32,15,256]{3,1,2,0:T(8,128)S(1)}, u32[]{:S(2)}, u32[]{:S(2)}) %collective-permute-start.8) | collective-permute-done | bytes 983072 | tf_op jit(solution)/shard_map/ppermute | solution.py:19
  289.1 21.2 %collective-permute-done.9 = f32[2,32,15,256]{3,1,2,0:T(8,128)S(1)} collective-permute-done((f32[2,32,15,256]{3,1,2,0:T(8,128)S(1)}, f32[2,32,15,256]{3,1,2,0:T(8,128)S(1)}, u32[]{:S(2)}, u32[]{:S(2)}) %collective-permute-start.9) | collective-permute-done | bytes 983072 | tf_op jit(solution)/shard_map/ppermute | solution.py:22
  310.9 4.5 %fusion.64 = f32[2,32,32,256]{3,2,1,0:T(8,128)S(1)} fusion(f32[2,32,62,256]{3,1,2,0:T(8,128)S(1)} %pad_maximum_fusion.2, f32[2,62,32,1]{1,0,2,3:T(2,128)S(1)} %convolution_bitcast_fusion.1), kind=kOutput, calls=%fused_computation.62 | convolution fusion | flops 390070272 | bytes 6176256 | tf_op jit(solution)/shard_map/czjy,cji->cziy/dot_general | solution.py:51
  319.4 5.7 %collective-permute-start.10 = (f32[2,32,32,15]{2,1,3,0:T(8,128)}, f32[2,32,32,15]{2,1,3,0:T(8,128)}, u32[]{:S(2)}, u32[]{:S(2)}) collective-permute-start(f32[2,32,32,15]{2,1,3,0:T(8,128)} %copy.44), channel_id=1, source_target_pairs={{0,4},{4,8},{8,12},{12,16},{16,20},{20,24},{24,28},{1,5},{5,9},{9,... | collective-permute-start | bytes 368648 | tf_op jit(solution)/shard_map/ppermute | solution.py:19
  332.6 4.3 collective-permute-done.11
  341.9 5.5 %fusion.23 = f32[2,32,32,256]{3,1,2,0:T(8,128)S(1)} fusion(f32[2,32,32,286]{3,2,1,0:T(8,128)S(1)} %pad_maximum_fusion.6, f32[2,286,256,1]{2,0,1,3:T(2,128)S(1)} %copy-done.8), kind=kOutput, calls=%fused_computation.34 | convolution fusion | flops 1799356416 | bytes 5025792 | tf_op jit(solution)/shard_map/czxj,cji->czxi/dot_general | solution.py:55
  347.4 3.1 fusion.45
  353.6 13.9 %collective-permute-done.12 = f32[2,32,15,256]{3,1,2,0:T(8,128)S(1)} collective-permute-done((f32[2,32,15,256]{3,1,2,0:T(8,128)S(1)}, f32[2,32,15,256]{3,1,2,0:T(8,128)S(1)}, u32[]{:S(2)}, u32[]{:S(2)}) %collective-permute-start.12) | collective-permute-done | bytes 983072 | tf_op jit(solution)/shard_map/ppermute | solution.py:19
  367.5 21.2 %collective-permute-done.13 = f32[2,32,15,256]{3,1,2,0:T(8,128)S(1)} collective-permute-done((f32[2,32,15,256]{3,1,2,0:T(8,128)S(1)}, f32[2,32,15,256]{3,1,2,0:T(8,128)S(1)}, u32[]{:S(2)}, u32[]{:S(2)}) %collective-permute-start.13) | collective-permute-done | bytes 983072 | tf_op jit(solution)/shard_map/ppermute | solution.py:22
  389.3 4.5 %fusion.67 = f32[2,32,32,256]{3,2,1,0:T(8,128)S(1)} fusion(f32[2,32,62,256]{3,1,2,0:T(8,128)S(1)} %pad_maximum_fusion.3, f32[2,62,32,1]{1,0,2,3:T(2,128)S(1)} %convolution_bitcast_fusion.3), kind=kOutput, calls=%fused_computation.63 | convolution fusion | flops 390070272 | bytes 6176256 | tf_op jit(solution)/shard_map/czjy,cji->cziy/dot_general | solution.py:51
  397.8 7.5 %collective-permute-start.14 = (f32[2,32,32,15]{2,1,3,0:T(8,128)}, f32[2,32,32,15]{2,1,3,0:T(8,128)}, u32[]{:S(2)}, u32[]{:S(2)}) collective-permute-start(f32[2,32,32,15]{2,1,3,0:T(8,128)} %copy.51), channel_id=1, source_target_pairs={{0,4},{4,8},{8,12},{12,16},{16,20},{20,24},{24,28},{1,5},{5,9},{9,... | collective-permute-start | bytes 368648 | tf_op jit(solution)/shard_map/ppermute | solution.py:19
  412.8 4.3 collective-permute-done.15
  422.1 5.5 %fusion.55 = f32[2,32,32,256]{3,1,2,0:T(8,128)S(1)} fusion(f32[2,32,32,256]{3,1,2,0:T(8,128)S(1)} %copy-done.5, f32[2,32,32,286]{3,2,1,0:T(8,128)S(1)} %pad_maximum_fusion.7, f32[2,286,256,1]{2,0,1,3:T(2,128)S(1)} %copy-done.10), kind=kOutput, calls=%fused_computation.59 | convolution fusion | flops 1799880704 | bytes 7122944 | tf_op jit(solution)/shard_map/czxj,cji->czxi/dot_general | solution.py:55
  (108 shorter events, 97.8 us)
Async XLA Ops:
  0.1 8.0 %copy-start.11 = (f32[2,1,128,2048]{3,2,1,0:T(8,128)S(1)}, f32[2,1,128,2048]{3,2,1,0:T(8,128)}, u32[]{:S(2)}) copy-start(f32[2,1,128,2048]{3,2,1,0:T(8,128)} %param.2) | copy-start | bytes 6291460
  36.2 7.1 %copy-start.15 = (f32[3,2,31]{2,1,0:T(2,128)S(1)}, f32[3,2,31]{2,1,0:T(2,128)}, u32[]{:S(2)}) copy-start(f32[3,2,31]{2,1,0:T(2,128)} %param.3) | copy-start | bytes 2236
  36.2 55.1 %all-to-all-start = ((f32[32,2,1,32,256]{4,3,1,2,0:T(8,128)}), f32[32,2,1,32,256]{4,3,1,2,0:T(8,128)S(1)}, u32[]{:S(2)}, u32[]{:S(2)}) async-start(f32[32,2,1,32,256]{4,3,1,2,0:T(8,128)} %bitcast.112), calls=%async_computation | async-start | bytes 4194304 | tf_op jit(solution)/shard_map/all_to_all | solution.py:91
  43.5 59.0 %copy-start.14 = (f32[3,2,31]{2,1,0:T(2,128)}, f32[3,2,31]{2,1,0:T(2,128)S(1)}, u32[]{:S(2)}) copy-start(f32[3,2,31]{2,1,0:T(2,128)S(1)} %broadcast_divide_fusion) | copy-start | bytes 2236
  91.3 4.3 copy-start
  95.9 23.6 %collective-permute-start = (f32[2,32,15,256]{3,1,2,0:T(8,128)}, f32[2,32,15,256]{3,1,2,0:T(8,128)S(1)}, u32[]{:S(2)}, u32[]{:S(2)}) collective-permute-start(f32[2,32,15,256]{3,1,2,0:T(8,128)} %get-tuple-element.19), channel_id=1, source_target_pairs={{0,1},{1,2},{2,3},{4,5},{5,6},{6,7},{8,9},{9,10},{10,11},{12,13},{... | collective-permute-start | bytes 2949128 | tf_op jit(solution)/shard_map/ppermute | solution.py:19
  99.2 44.0 %collective-permute-start.1 = (f32[2,32,15,256]{3,1,2,0:T(8,128)S(1)}, f32[2,32,15,256]{3,1,2,0:T(8,128)S(1)}, u32[]{:S(2)}, u32[]{:S(2)}) collective-permute-start(f32[2,32,15,256]{3,1,2,0:T(8,128)S(1)} %get-tuple-element.20), channel_id=1, source_target_pairs={{1,0},{2,1},{3,2},{5,4},{6,5},{7,6},{9,8},{10,9},{11,10},{13,12},{... | collective-permute-start | bytes 2949128 | tf_op jit(solution)/shard_map/ppermute | solution.py:22
  102.4 76.1 %copy-start.12 = (f32[2,32,32,1]{1,2,3,0:T(8,128)}, f32[2,32,32,1]{1,2,3,0:T(8,128)S(1)}, u32[]{:S(2)}) copy-start(f32[2,32,32,1]{1,2,3,0:T(8,128)S(1)} %copy.62) | copy-start | bytes 24580
  154.9 13.1 %collective-permute-start.3 = (f32[2,32,32,15]{2,1,3,0:T(8,128)}, f32[2,32,32,15]{2,1,3,0:T(8,128)}, u32[]{:S(2)}, u32[]{:S(2)}) collective-permute-start(f32[2,32,32,15]{2,1,3,0:T(8,128)} %copy.29), channel_id=1, source_target_pairs={{4,0},{8,4},{12,8},{16,12},{20,16},{24,20},{28,24},{5,1},{9,5},{13... | collective-permute-start | bytes 368648 | tf_op jit(solution)/shard_map/ppermute | solution.py:22
  158.3 8.3 %collective-permute-start.2 = (f32[2,32,32,15]{2,1,3,0:T(8,128)}, f32[2,32,32,15]{2,1,3,0:T(8,128)}, u32[]{:S(2)}, u32[]{:S(2)}) collective-permute-start(f32[2,32,32,15]{2,1,3,0:T(8,128)} %copy.28), channel_id=1, source_target_pairs={{0,4},{4,8},{8,12},{12,16},{16,20},{20,24},{24,28},{1,5},{5,9},{9,... | collective-permute-start | bytes 368648 | tf_op jit(solution)/shard_map/ppermute | solution.py:19
  173.0 5.6 %copy-start.1 = (f32[32,2,1,32,256]{4,3,1,2,0:T(8,128)S(1)}, f32[32,2,1,32,256]{4,3,1,2,0:T(8,128)}, u32[]{:S(2)}) copy-start(f32[32,2,1,32,256]{4,3,1,2,0:T(8,128)} %copy-done) | copy-start | bytes 6291460
  181.9 5.8 %copy-start.17 = (f32[1,2,31]{2,1,0:T(2,128)S(1)}, f32[1,2,31]{2,1,0:T(2,128)}, u32[]{:S(2)}) copy-start(f32[1,2,31]{2,1,0:T(2,128)} %get-tuple-element.21) | copy-start | bytes 748
  181.9 6.5 %copy-start.16 = (f32[1,2,31]{2,1,0:T(2,128)S(1)}, f32[1,2,31]{2,1,0:T(2,128)}, u32[]{:S(2)}) copy-start(f32[1,2,31]{2,1,0:T(2,128)} %get-tuple-element.23) | copy-start | bytes 748
  183.0 24.0 %collective-permute-start.4 = (f32[2,32,15,256]{3,1,2,0:T(8,128)}, f32[2,32,15,256]{3,1,2,0:T(8,128)}, u32[]{:S(2)}, u32[]{:S(2)}) collective-permute-start(f32[2,32,15,256]{3,1,2,0:T(8,128)} %get-tuple-element.15), channel_id=1, source_target_pairs={{0,1},{1,2},{2,3},{4,5},{5,6},{6,7},{8,9},{9,10},{10,11},{12,13},{... | collective-permute-start | bytes 2949128 | tf_op jit(solution)/shard_map/ppermute | solution.py:19
  186.4 42.7 %collective-permute-start.5 = (f32[2,32,15,256]{3,1,2,0:T(8,128)S(1)}, f32[2,32,15,256]{3,1,2,0:T(8,128)}, u32[]{:S(2)}, u32[]{:S(2)}) collective-permute-start(f32[2,32,15,256]{3,1,2,0:T(8,128)S(1)} %get-tuple-element.16), channel_id=1, source_target_pairs={{1,0},{2,1},{3,2},{5,4},{6,5},{7,6},{9,8},{10,9},{11,10},{13,12},{... | collective-permute-start | bytes 2949128 | tf_op jit(solution)/shard_map/ppermute | solution.py:22
  235.5 11.3 %copy-start.18 = (f32[1,2,31]{2,1,0:T(2,128)S(1)}, f32[1,2,31]{2,1,0:T(2,128)}, u32[]{:S(2)}) copy-start(f32[1,2,31]{2,1,0:T(2,128)} %slice.88) | copy-start | bytes 748
  240.8 13.1 %collective-permute-start.7 = (f32[2,32,32,15]{2,1,3,0:T(8,128)}, f32[2,32,32,15]{2,1,3,0:T(8,128)}, u32[]{:S(2)}, u32[]{:S(2)}) collective-permute-start(f32[2,32,32,15]{2,1,3,0:T(8,128)} %copy.36), channel_id=1, source_target_pairs={{4,0},{8,4},{12,8},{16,12},{20,16},{24,20},{28,24},{5,1},{9,5},{13... | collective-permute-start | bytes 368648 | tf_op jit(solution)/shard_map/ppermute | solution.py:22
  243.1 9.3 %collective-permute-start.6 = (f32[2,32,32,15]{2,1,3,0:T(8,128)}, f32[2,32,32,15]{2,1,3,0:T(8,128)}, u32[]{:S(2)}, u32[]{:S(2)}) collective-permute-start(f32[2,32,32,15]{2,1,3,0:T(8,128)} %copy.35), channel_id=1, source_target_pairs={{0,4},{4,8},{8,12},{12,16},{16,20},{20,24},{24,28},{1,5},{5,9},{9,... | collective-permute-start | bytes 368648 | tf_op jit(solution)/shard_map/ppermute | solution.py:19
  256.4 2.5 copy-start.2
  256.4 2.5 copy-start.9
  267.9 21.3 %collective-permute-start.8 = (f32[2,32,15,256]{3,1,2,0:T(8,128)S(1)}, f32[2,32,15,256]{3,1,2,0:T(8,128)S(1)}, u32[]{:S(2)}, u32[]{:S(2)}) collective-permute-start(f32[2,32,15,256]{3,1,2,0:T(8,128)S(1)} %get-tuple-element.11), channel_id=1, source_target_pairs={{0,1},{1,2},{2,3},{4,5},{5,6},{6,7},{8,9},{9,10},{10,11},{12,13},{... | collective-permute-start | bytes 2949128 | tf_op jit(solution)/shard_map/ppermute | solution.py:19
  269.2 41.2 %collective-permute-start.9 = (f32[2,32,15,256]{3,1,2,0:T(8,128)S(1)}, f32[2,32,15,256]{3,1,2,0:T(8,128)S(1)}, u32[]{:S(2)}, u32[]{:S(2)}) collective-permute-start(f32[2,32,15,256]{3,1,2,0:T(8,128)S(1)} %get-tuple-element.12), channel_id=1, source_target_pairs={{1,0},{2,1},{3,2},{5,4},{6,5},{7,6},{9,8},{10,9},{11,10},{13,12},{... | collective-permute-start | bytes 2949128 | tf_op jit(solution)/shard_map/ppermute | solution.py:22
  319.4 11.7 %collective-permute-start.10 = (f32[2,32,32,15]{2,1,3,0:T(8,128)}, f32[2,32,32,15]{2,1,3,0:T(8,128)}, u32[]{:S(2)}, u32[]{:S(2)}) collective-permute-start(f32[2,32,32,15]{2,1,3,0:T(8,128)} %copy.44), channel_id=1, source_target_pairs={{0,4},{4,8},{8,12},{12,16},{16,20},{20,24},{24,28},{1,5},{5,9},{9,... | collective-permute-start | bytes 368648 | tf_op jit(solution)/shard_map/ppermute | solution.py:19
  326.5 10.5 %collective-permute-start.11 = (f32[2,32,32,15]{2,1,3,0:T(8,128)}, f32[2,32,32,15]{2,1,3,0:T(8,128)}, u32[]{:S(2)}, u32[]{:S(2)}) collective-permute-start(f32[2,32,32,15]{2,1,3,0:T(8,128)} %copy.45), channel_id=1, source_target_pairs={{4,0},{8,4},{12,8},{16,12},{20,16},{24,20},{28,24},{5,1},{9,5},{13... | collective-permute-start | bytes 368648 | tf_op jit(solution)/shard_map/ppermute | solution.py:22
  341.8 5.6 %copy-start.3 = (f32[32,2,1,32,256]{4,3,1,2,0:T(8,128)S(1)}, f32[32,2,1,32,256]{4,3,1,2,0:T(8,128)}, u32[]{:S(2)}) copy-start(f32[32,2,1,32,256]{4,3,1,2,0:T(8,128)} %copy-done) | copy-start | bytes 6291460
  341.9 5.6 %copy-start.13 = (f32[2,32,32,1]{1,2,3,0:T(8,128)S(1)}, f32[2,32,32,1]{1,2,3,0:T(8,128)}, u32[]{:S(2)}) copy-start(f32[2,32,32,1]{1,2,3,0:T(8,128)} %copy-done.12) | copy-start | bytes 24580
  350.7 16.8 %collective-permute-start.12 = (f32[2,32,15,256]{3,1,2,0:T(8,128)S(1)}, f32[2,32,15,256]{3,1,2,0:T(8,128)S(1)}, u32[]{:S(2)}, u32[]{:S(2)}) collective-permute-start(f32[2,32,15,256]{3,1,2,0:T(8,128)S(1)} %get-tuple-element.7), channel_id=1, source_target_pairs={{0,1},{1,2},{2,3},{4,5},{5,6},{6,7},{8,9},{9,10},{10,11},{12,13},{... | collective-permute-start | bytes 2949128 | tf_op jit(solution)/shard_map/ppermute | solution.py:19
  352.1 36.7 %collective-permute-start.13 = (f32[2,32,15,256]{3,1,2,0:T(8,128)S(1)}, f32[2,32,15,256]{3,1,2,0:T(8,128)S(1)}, u32[]{:S(2)}, u32[]{:S(2)}) collective-permute-start(f32[2,32,15,256]{3,1,2,0:T(8,128)S(1)} %get-tuple-element.8), channel_id=1, source_target_pairs={{1,0},{2,1},{3,2},{5,4},{6,5},{7,6},{9,8},{10,9},{11,10},{13,12},{... | collective-permute-start | bytes 2949128 | tf_op jit(solution)/shard_map/ppermute | solution.py:22
  397.8 13.6 %collective-permute-start.14 = (f32[2,32,32,15]{2,1,3,0:T(8,128)}, f32[2,32,32,15]{2,1,3,0:T(8,128)}, u32[]{:S(2)}, u32[]{:S(2)}) collective-permute-start(f32[2,32,32,15]{2,1,3,0:T(8,128)} %copy.51), channel_id=1, source_target_pairs={{0,4},{4,8},{8,12},{12,16},{16,20},{20,24},{24,28},{1,5},{5,9},{9,... | collective-permute-start | bytes 368648 | tf_op jit(solution)/shard_map/ppermute | solution.py:19
  406.6 10.5 %collective-permute-start.15 = (f32[2,32,32,15]{2,1,3,0:T(8,128)}, f32[2,32,32,15]{2,1,3,0:T(8,128)}, u32[]{:S(2)}, u32[]{:S(2)}) collective-permute-start(f32[2,32,32,15]{2,1,3,0:T(8,128)} %copy.52), channel_id=1, source_target_pairs={{4,0},{8,4},{12,8},{16,12},{20,16},{24,20},{28,24},{5,1},{9,5},{13... | collective-permute-start | bytes 368648 | tf_op jit(solution)/shard_map/ppermute | solution.py:22
  419.5 2.5 copy-start.5
  419.5 2.5 copy-start.10
  (4 other events, 8.8 us)
where the time goes:
time: 435 us; the launch traced here: 431 us
  waiting for transfers between devices  219 us (50%)
  matrix products  89.1 us (20%)
  starting transfers between devices  51 us (12%)
  local copies, waits for them, and re-layouts  47.1 us (11%)
  other arithmetic  23.2 us (5%)
    ppermute x8, waiting for transfers between devices, padded(): lax.ppermute(lax.slice_in_dim(block, 0, width, axis=dim), axis, backward)  96.7 us
    ppermute x8, waiting for transfers between devices, padded(): lax.ppermute(lax.slice_in_dim(block, block.shape[dim] - width, None, axis...  75.9 us
    all_to_all x1, waiting for transfers between devices, local(): lax.all_to_all(blocks, ('gx', 'gy'), split_axis=0, concat_axis=2, tiled=T...  46.5 us
    ppermute x8, starting transfers between devices, padded(): lax.ppermute(lax.slice_in_dim(block, block.shape[dim] - width, None, axis...  28.5 us
    dot_general x1, matrix products, local(): jnp.einsum('czxj,jy->czxy', smoothed, along_table, precision=lax.Precisio...  23.3 us
    dot_general x4, matrix products, along_lines(): jnp.einsum('czxj,cji->czxi', volume, matrix, precision=lax.Precision.HIGH...  23.2 us
    slice x12, local copies, waits for them, and re-layouts, padded(): lax.slice_in_dim(block, block.shape[dim] - width, None, axis=dim)  18.4 us
    dot_general x4, matrix products, along_rows(): jnp.einsum('czjy,cji->cziy', volume, matrix, precision=lax.Precision.HIGH...  17.9 us
  transfers between devices with their start and end apart: 17, of which 15 were waited for; matrix products, arithmetic and copies ran while one was open for 5% of the time, Pallas kernels for 0%

commit v1 on v0

v1 whole, which is shorter than its diff:
```python
import functools

import jax
import jax.numpy as jnp
from jax import lax
from jax.experimental import pallas as pl
from jax.experimental.pallas import tpu as pltpu
from jax.sharding import PartitionSpec as P

ITERS = 2
BACKGROUND = 0.5
SIGMA_ACROSS = 48.0
SIGMA_ALONG = 96.0
SUB = 8
CHUNKS = 4
MESH = pl.DeviceIdType.MESH


def smoothing_table(length_cells, spread_cells, circular):
    places = lax.iota(jnp.int32, length_cells)
    offset = jnp.abs(places[:, None] - places[None, :])
    if circular:
        offset = jnp.minimum(offset, length_cells - offset)
    scaled = offset.astype(jnp.float32) / spread_cells
    kernel_table = jnp.exp(-0.5 * scaled * scaled)
    return kernel_table / jnp.sum(kernel_table, axis=1, keepdims=True)


def halves(table):
    high = lax.reduce_precision(table, 8, 7)
    return high.astype(jnp.bfloat16), (table - high).astype(jnp.bfloat16)


def banded(taps, lag, mask=None):
    table = jnp.zeros(lag.shape, jnp.float32)
    for k in range(taps.shape[0]):
        hit = lag == k
        table = jnp.where(hit if mask is None else hit & mask, taps[k], table)
    return table


def depth_table(taps, planes):
    size = planes * SUB
    row = lax.broadcasted_iota(jnp.int32, (size, size), 0)
    col = lax.broadcasted_iota(jnp.int32, (size, size), 1)
    lag = col // SUB - row // SUB + taps.shape[0] // 2
    return jnp.concatenate(halves(banded(taps, lag, row % SUB == col % SUB)), axis=0)


def rows_table(taps, lines):
    row = lax.broadcasted_iota(jnp.int32, (lines, lines), 0)
    col = lax.broadcasted_iota(jnp.int32, (lines, lines), 1)
    both = jnp.concatenate(halves(banded(taps, row - col + taps.shape[0] // 2)), axis=1)
    return jnp.concatenate([both, both], axis=0)


def lines_table(taps, cells, edge):
    row = lax.broadcasted_iota(jnp.int32, (cells, cells + 2 * edge), 0)
    col = lax.broadcasted_iota(jnp.int32, (cells, cells + 2 * edge), 1)
    lag = col - row - edge + taps.shape[0] // 2
    return jnp.concatenate(halves(banded(taps, lag)), axis=0)


def split(value):
    high = value.astype(jnp.bfloat16)
    low = (value - high.astype(jnp.float32)).astype(jnp.bfloat16)
    return jnp.concatenate([high, low], axis=1)


def place_of(count_gy, pair, gy):
    first = gy // 2
    along = 2 * first + (gy % 2 + first) % 2
    odd = pair % 2
    return (1 - odd) * along + odd * (count_gy - 1 - along)


def device_of(count_gy, line):
    pair, place = line // count_gy, line % count_gy
    odd = pair % 2
    along = (1 - odd) * place + odd * (count_gy - 1 - place)
    first = along // 2
    return pair, 2 * first + (along % 2 + first) % 2


def deconvolve_kernel(
    count_gx, count_gy, edge, cleaned, depth, rows, lines, out,
    estimate, ratio, wide, stage, send_sem, recv_sem, out_send, out_recv, own_sem,
):
    planes, cells, width = cleaned.shape
    size = planes * SUB
    gx, gy = lax.axis_index("gx"), lax.axis_index("gy")
    pair, core = gx // 2, gx % 2
    place = place_of(count_gy, pair, gy)
    line = pair * count_gy + place
    last = count_gx // 2 * count_gy - 1
    per_gx = count_gy // 2
    lines_x = width // count_gy
    me = gx * count_gy + gy

    barrier = pltpu.get_barrier_semaphore()

    @pl.loop(0, count_gx * count_gy)
    def _(other):
        @pl.when(other != me)
        def _():
            pl.semaphore_signal(
                barrier, inc=1, device_id=(other // count_gy, other % count_gy), device_id_type=MESH
            )

    pl.semaphore_wait(barrier, count_gx * count_gy - 1)

    zeros = jnp.zeros((planes, edge, width), jnp.float32)

    @pl.when(line == 0)
    def _():
        for slot in range(2):
            wide[slot, :, 0:edge, :] = zeros

    @pl.when(line == last)
    def _():
        for slot in range(2):
            wide[slot, :, edge + cells :, :] = zeros

    def edge_copy(slot, up):
        target_pair, target_gy = device_of(count_gy, line + (1 if up else -1))
        source = cells if up else edge
        target = 0 if up else edge + cells
        side = 1 if up else 0
        return pltpu.make_async_remote_copy(
            src_ref=wide.at[slot, :, pl.ds(source, edge), :],
            dst_ref=wide.at[slot, :, pl.ds(target, edge), :],
            send_sem=send_sem.at[slot, side],
            recv_sem=recv_sem.at[slot, side],
            device_id=(target_pair * 2 + core, target_gy),
            device_id_type=MESH,
        )

    def planes_and_rows(field, slot, way, group):
        start = pl.multiple_of(group * SUB, SUB)
        value = field[:, pl.ds(start, SUB), :].reshape(size, width)
        value = jnp.dot(depth[way], split(value), preferred_element_type=jnp.float32)
        value = value[:size] + value[size:]
        value = value[:, :width] + value[:, width:]
        value = jnp.dot(split(value), rows[way], preferred_element_type=jnp.float32)
        value = value[:, :width] + value[:, width:]
        wide[slot, :, pl.ds(edge + start, SUB), :] = value.reshape(planes, SUB, width)

    def along_lines(slot, way, plane):
        value = jnp.dot(lines[way], split(wide[slot, plane]), preferred_element_type=jnp.float32)
        value = value[:cells] + value[cells:]
        return value[:, :width] + value[:, width:]

    def spread(field, slot, way):
        groups = cells // SUB
        outer = edge // SUB

        for group in range(outer):
            planes_and_rows(field, slot, way, group)

        @pl.when(line > 0)
        def _():
            edge_copy(slot, False).start()

        for group in range(groups - outer, groups):
            planes_and_rows(field, slot, way, group)

        @pl.when(line < last)
        def _():
            edge_copy(slot, True).start()

        if groups > 2 * outer:

            @pl.loop(outer, groups - outer)
            def _(group):
                planes_and_rows(field, slot, way, group)

        @pl.when(line > 0)
        def _():
            edge_copy(slot, False).wait_send()
            edge_copy(slot, True).wait_recv()

        @pl.when(line < last)
        def _():
            edge_copy(slot, True).wait_send()
            edge_copy(slot, False).wait_recv()

    def out_copy(chunk, target_gy):
        part = pl.ds(chunk * (planes // CHUNKS), planes // CHUNKS)
        return pltpu.make_async_remote_copy(
            src_ref=stage.at[target_gy, part],
            dst_ref=out.at[core, place % per_gx, part],
            send_sem=out_send.at[chunk, target_gy],
            recv_sem=out_recv.at[chunk, core, place % per_gx],
            device_id=(pair * 2 + place // per_gx, target_gy),
            device_id_type=MESH,
        )

    def own_copy(chunk):
        part = pl.ds(chunk * (planes // CHUNKS), planes // CHUNKS)
        return pltpu.make_async_copy(
            stage.at[gy, part], out.at[core, place % per_gx, part], own_sem.at[chunk]
        )

    def is_own(target_gy):
        return jnp.logical_and(target_gy == gy, place // per_gx == core)

    for iteration in range(ITERS):
        source = cleaned if iteration == 0 else estimate
        spread(source, 0, 0)

        @pl.loop(0, planes, unroll=2)
        def _(plane):
            ratio[plane] = cleaned[plane] / (along_lines(0, 0, plane) + BACKGROUND)

        spread(ratio, 1, 1)
        if iteration < ITERS - 1:

            @pl.loop(0, planes, unroll=2)
            def _(plane):
                estimate[plane] = source[plane] * along_lines(1, 1, plane)

        else:
            for chunk in range(CHUNKS):

                @pl.loop(chunk * (planes // CHUNKS), (chunk + 1) * (planes // CHUNKS), unroll=2)
                def _(plane):
                    value = (source[plane] * along_lines(1, 1, plane)).T
                    for target in range(count_gy):
                        stage[target, plane] = value[target * lines_x : (target + 1) * lines_x]

                for target in range(count_gy):

                    @pl.when(is_own(target))
                    def _():
                        own_copy(chunk).start()

                    @pl.when(jnp.logical_not(is_own(target)))
                    def _():
                        out_copy(chunk, target).start()

    for chunk in range(CHUNKS):
        part = pl.ds(chunk * (planes // CHUNKS), planes // CHUNKS)
        for target in range(count_gy):

            @pl.when(is_own(target))
            def _():
                own_copy(chunk).wait()

            @pl.when(jnp.logical_not(is_own(target)))
            def _():
                out_copy(chunk, target).wait_send()

        for channel in range(2):
            for slot in range(per_gx):
                mine = jnp.logical_and(channel == core, place == core * per_gx + slot)

                @pl.when(jnp.logical_not(mine))
                def _():
                    pltpu.make_async_remote_copy(
                        src_ref=stage.at[0, part],
                        dst_ref=out.at[channel, slot, part],
                        send_sem=out_send.at[chunk, 0],
                        recv_sem=out_recv.at[chunk, channel, slot],
                        device_id=(gx, gy),
                        device_id_type=MESH,
                    ).wait_recv()


def local(raw_stack, psf_taps):
    channels, own_planes, lines_x, lines_y = raw_stack.shape
    half_taps = psf_taps.shape[2] // 2
    count_gx = lax.axis_size("gx")
    count_gy = lax.axis_size("gy")
    pairs = count_gx // channels
    cells = lines_y // (pairs * count_gy)
    planes = own_planes * count_gx * count_gy
    edge = -(-half_taps // SUB) * SUB

    across_table = smoothing_table(lines_x, SIGMA_ACROSS, False)
    along_table = smoothing_table(lines_y, SIGMA_ALONG, True)
    smoothed = jnp.einsum("ij,czjy->cziy", across_table, raw_stack, precision=lax.Precision.HIGH)
    stripes = smoothed - jnp.einsum(
        "czxj,jy->czxy", smoothed, along_table, precision=lax.Precision.HIGH
    )
    cleaned_plane = jnp.maximum(raw_stack - stripes, 0.0)

    blocks = cleaned_plane.reshape(channels, own_planes, lines_x, pairs, count_gy, cells)
    blocks = jnp.transpose(blocks, (3, 0, 4, 1, 5, 2))
    ordered = []
    for pair in range(pairs):
        order = [place_of(count_gy, pair, gy) for gy in range(count_gy)]
        ordered.append(jnp.stack([blocks[pair, :, place] for place in order], axis=1))
    blocks = jnp.stack(ordered).reshape(count_gx * count_gy * own_planes, cells, lines_x)
    cleaned = lax.all_to_all(blocks, ("gx", "gy"), split_axis=0, concat_axis=0, tiled=True)

    channel = lax.axis_index("gx") % channels
    taps = jnp.where(channel == 0, psf_taps[:, 0], psf_taps[:, 1])
    forward = taps / jnp.sum(taps, axis=1, keepdims=True)
    both = (forward, forward[:, ::-1])
    depth = jnp.stack([depth_table(q[0], planes) for q in both])
    rows = jnp.stack([rows_table(q[1], lines_x) for q in both])
    lines = jnp.stack([lines_table(q[2], cells, edge) for q in both])

    per_gx = count_gy // 2
    block_x = lines_x // count_gy
    field = pltpu.VMEM((planes, cells, lines_x), jnp.float32)
    vmem = pl.BlockSpec(memory_space=pltpu.VMEM)
    gathered = pl.pallas_call(
        functools.partial(deconvolve_kernel, count_gx, count_gy, edge),
        out_shape=jax.ShapeDtypeStruct((channels, per_gx, planes, block_x, cells), jnp.float32),
        in_specs=[vmem] * 4,
        out_specs=pl.BlockSpec(memory_space=pl.ANY),
        scratch_shapes=[
            field,
            field,
            pltpu.VMEM((2, planes, cells + 2 * edge, lines_x), jnp.float32),
            pltpu.VMEM((count_gy, planes, block_x, cells), jnp.float32),
            pltpu.SemaphoreType.DMA((2, 2)),
            pltpu.SemaphoreType.DMA((2, 2)),
            pltpu.SemaphoreType.DMA((CHUNKS, count_gy)),
            pltpu.SemaphoreType.DMA((CHUNKS, channels, per_gx)),
            pltpu.SemaphoreType.DMA((CHUNKS,)),
        ],
        compiler_params=pltpu.CompilerParams(
            collective_id=0, has_side_effects=True, vmem_limit_bytes=60 * 1024 * 1024
        ),
    )(cleaned, depth, rows, lines)
    return jnp.transpose(gathered, (0, 2, 3, 1, 4)).reshape(
        channels, planes, block_x, per_gx * cells
    )


def solution(mesh):
    in_specs = (P(None, ("gx", "gy"), None, None), P())
    out_specs = P(None, None, "gy", "gx")
    return jax.shard_map(local, mesh=mesh, in_specs=in_specs, out_specs=out_specs, check_vma=False)
```

time: 435 us -> 363 us (0.83)
  other arithmetic: 23.2 us -> 251 us
  waiting for transfers between devices: 219 us -> 0.01 us
  matrix products: 89.1 us -> 14.5 us
  Pallas kernels: 0 us -> 73.7 us
  starting transfers between devices: 51 us -> 7.08 us
  local copies, waits for them, and re-layouts: 47.1 us -> 12.6 us
    convert_element_type x0 -> x12, other arithmetic: none -> 239 us  [halves(): return (high.astype(jnp.bfloat16), (table - high).astype(jnp.bfloat16))]
    ppermute x16 -> x0, waiting for transfers between devices: 173 us -> none  [the longest x8 96.7 us: padded(): lax.ppermute(lax.slice_in_dim(block, 0, width, axis=dim), axis, backward)]
    pallas_call x0 -> x1, Pallas kernels: none -> 73.7 us  [local(): pl.pallas_call(functools.partial(deconvolve_kernel, count_gx, count_gy, e...]
    dot_general x18 -> x0, matrix products: 63.9 us -> none  [the longest x4 23.2 us: along_lines(): jnp.einsum('czxj,cji->czxi', volume, matrix, precision=lax.Precision.HIGH...]
    all_to_all x1, waiting for transfers between devices: 46.5 us -> 0.01 us  [local(): lax.all_to_all(blocks, ('gx', 'gy'), split_axis=0, concat_axis=0, tiled=T...]
    ppermute x16 -> x0, starting transfers between devices: 43.9 us -> none  [the longest x8 28.5 us: padded(): lax.ppermute(lax.slice_in_dim(block, block.shape[dim] - width, None, axis...]
    slice x20 -> x5, local copies, waits for them, and re-layouts: 25.3 us -> 3.63 us  [banded(): table = jnp.where(hit if mask is None else hit & mask, taps[k], table)]
    ppermute x8 -> x0, local copies, waits for them, and re-layouts: 15.8 us -> none  [the longest x4 9.84 us: padded(): lax.ppermute(lax.slice_in_dim(block, 0, width, axis=dim), axis, backward)]
  transfers between devices with their start and end apart: 17 -> 1, of which waited for: 15 -> 0; matrix products, arithmetic and copies ran while one was open for 5% -> 68% of each run, Pallas kernels for 0% -> 0%
where the time goes in v1:
time: 363 us; the launch traced here: 360 us
  other arithmetic  251 us (69%)
  Pallas kernels  73.7 us (20%)
  matrix products  14.5 us (4%)
  local copies, waits for them, and re-layouts  12.6 us (3%)
  starting transfers between devices  7.08 us (2%)
    convert_element_type x12, other arithmetic, halves(): return (high.astype(jnp.bfloat16), (table - high).astype(jnp.bfloat16))  239 us
    pallas_call x1, Pallas kernels, local(): pl.pallas_call(functools.partial(deconvolve_kernel, count_gx, count_gy, e...  73.7 us
    dot_general x1, matrix products, local(): jnp.einsum('czxj,jy->czxy', smoothed, along_table, precision=lax.Precisio...  13.4 us
    reduce_sum x2, other arithmetic, smoothing_table(): return kernel_table / jnp.sum(kernel_table, axis=1, keepdims=True)  8.11 us
  transfers between devices with their start and end apart: 1, of which 0 were waited for; matrix products, arithmetic and copies ran while one was open for 68% of the time, Pallas kernels for 0%

profile of v1, /device:TPU:1, one launch (start us, length us, event | category | flops | bytes accessed | tf_op | source)
XLA Modules:
  0.0 359.6 jit_solution(7966653669332967234)
XLA Ops:
  0.0 8.0 %fusion.4 = f32[2048]{0:T(1024)S(1)} fusion(), kind=kLoop, calls=%fused_computation.6 | loop fusion | flops 37746688 | bytes 8192 | tf_op jit(solution)/shard_map/reduce_sum | solution.py:26
  8.0 0.1 fusion.157
  8.1 1.1 fusion.22
  9.2 13.4 %fusion.18 = f32[2,1,128,2048]{3,2,0,1:T(8,128)S(1)} fusion(f32[2048]{0:T(1024)S(1)} %fusion.4, f32[128,2,2048]{2,0,1:T(8,128)S(1)} %fusion.22, f32[2,1,128,2048]{3,2,1,0:T(8,128)S(1)} %copy-done.1), kind=kOutput, calls=%fused_computation.14 | convolution fusion | flops 6481772544 | bytes 6299648 | tf_op jit(solution)/shard_map/czxj,jy->czxy/dot_general | solution.py:282
  22.6 2.4 reshape.396
  25.1 1.9 copy.12
  27.0 0.2 slice_bitcast_fusion.15
  27.4 1.5 pad_maximum_fusion
  28.8 7.1 %all-to-all-start = ((f32[32,128,128]{2,1,0:T(8,128)}), f32[32,128,128]{2,1,0:T(8,128)S(1)}, u32[]{:S(2)}, u32[]{:S(2)}) async-start(f32[32,128,128]{2,1,0:T(8,128)} %bitcast.35), calls=%async_computation | async-start | bytes 4194304 | tf_op jit(solution)/shard_map/all_to_all | solution.py:294
  36.2 0.7 fusion.172
  36.9 0.7 fusion.170
  37.6 0.7 fusion.171
  38.4 19.3 %fusion.121 = bf16[128,128]{1,0:T(8,128)(2,1)S(1)} fusion(f32[]{:T(128)} %bitcast.99, f32[]{:T(128)} %bitcast.98, f32[]{:T(128)} %bitcast.97, f32[]{:T(128)} %bitcast.96, f32[]{:T(128)} %bitcast.95, f32[]{:T(128)} %bitcast.94, f32[]{:T(128)} %bitcast.93, f32[]{:T(128)} %bitcast.92, f32[]{:T(128)} %bitcast.91, f32[]{:T(128)} %bitcast.90, f32[]{:T(128)} %bitcast.89, ...), kind=kLoop, calls=%fused_computation.165 | loop fusion | flops 1097728 | bytes 32892 | tf_op jit(solution)/shard_map/convert_element_type | solution.py:31
  57.7 19.3 %reduce-precision_convert_fusion.5 = bf16[128,128]{1,0:T(8,128)(2,1)S(1)} fusion(f32[]{:T(128)} %bitcast.99, f32[]{:T(128)} %bitcast.98, f32[]{:T(128)} %bitcast.97, f32[]{:T(128)} %bitcast.96, f32[]{:T(128)} %bitcast.95, f32[]{:T(128)} %bitcast.94, f32[]{:T(128)} %bitcast.93, f32[]{:T(128)} %bitcast.92, f32[]{:T(128)} %bitcast.91, f32[]{:T(128)} %bitcast.90, ...), kind=kLoop, calls=%fused_computation.164 | loop fusion | flops 1081344 | bytes 32892 | tf_op jit(solution)/shard_map/convert_element_type | solution.py:31
  77.0 19.3 %fusion.122 = bf16[128,128]{1,0:T(8,128)(2,1)S(1)} fusion(f32[]{:T(128)} %bitcast.69, f32[]{:T(128)} %bitcast.70, f32[]{:T(128)} %bitcast.71, f32[]{:T(128)} %bitcast.72, f32[]{:T(128)} %bitcast.73, f32[]{:T(128)} %bitcast.74, f32[]{:T(128)} %bitcast.75, f32[]{:T(128)} %bitcast.76, f32[]{:T(128)} %bitcast.77, f32[]{:T(128)} %bitcast.78, f32[]{:T(128)} %bitcast.79, ...), kind=kLoop, calls=%fused_computation.166 | loop fusion | flops 1097728 | bytes 32892 | tf_op jit(solution)/shard_map/convert_element_type | solution.py:31
  96.4 19.3 %reduce-precision_convert_fusion.4 = bf16[128,128]{1,0:T(8,128)(2,1)S(1)} fusion(f32[]{:T(128)} %bitcast.69, f32[]{:T(128)} %bitcast.70, f32[]{:T(128)} %bitcast.71, f32[]{:T(128)} %bitcast.72, f32[]{:T(128)} %bitcast.73, f32[]{:T(128)} %bitcast.74, f32[]{:T(128)} %bitcast.75, f32[]{:T(128)} %bitcast.76, f32[]{:T(128)} %bitcast.77, f32[]{:T(128)} %bitcast.78, ...), kind=kLoop, calls=%fused_computation.162 | loop fusion | flops 1081344 | bytes 32892 | tf_op jit(solution)/shard_map/convert_element_type | solution.py:31
  115.7 0.7 fusion.173
  116.4 0.7 fusion.169
  117.1 19.6 %fusion.88 = bf16[128,160]{1,0:T(8,128)(2,1)S(1)} fusion(f32[]{:T(128)} %bitcast.132, f32[]{:T(128)} %bitcast.131, f32[]{:T(128)} %bitcast.130, f32[]{:T(128)} %bitcast.129, f32[]{:T(128)} %bitcast.128, f32[]{:T(128)} %bitcast.127, f32[]{:T(128)} %bitcast.126, f32[]{:T(128)} %bitcast.125, f32[]{:T(128)} %bitcast.124, f32[]{:T(128)} %bitcast.123, ...), kind=kLoop, calls=%fused_computation.105 | loop fusion | flops 1372160 | bytes 41084 | tf_op jit(solution)/shard_map/convert_element_type | solution.py:31
  136.8 19.6 %reduce-precision_convert_fusion.3 = bf16[128,160]{1,0:T(8,128)(2,1)S(1)} fusion(f32[]{:T(128)} %bitcast.132, f32[]{:T(128)} %bitcast.131, f32[]{:T(128)} %bitcast.130, f32[]{:T(128)} %bitcast.129, f32[]{:T(128)} %bitcast.128, f32[]{:T(128)} %bitcast.127, f32[]{:T(128)} %bitcast.126, f32[]{:T(128)} %bitcast.125, f32[]{:T(128)} %bitcast.124, f32[]{:T(128)} %bitcast.123, ...), kind=kLoop, calls=%fused_computation.104 | loop fusion | flops 1351680 | bytes 41084 | tf_op jit(solution)/shard_map/convert_element_type | solution.py:31
  156.4 19.6 %fusion.89 = bf16[128,160]{1,0:T(8,128)(2,1)S(1)} fusion(f32[]{:T(128)} %bitcast.102, f32[]{:T(128)} %bitcast.103, f32[]{:T(128)} %bitcast.104, f32[]{:T(128)} %bitcast.105, f32[]{:T(128)} %bitcast.106, f32[]{:T(128)} %bitcast.107, f32[]{:T(128)} %bitcast.108, f32[]{:T(128)} %bitcast.109, f32[]{:T(128)} %bitcast.110, f32[]{:T(128)} %bitcast.111, ...), kind=kLoop, calls=%fused_computation.106 | loop fusion | flops 1372160 | bytes 41084 | tf_op jit(solution)/shard_map/convert_element_type | solution.py:31
  176.0 19.6 %reduce-precision_convert_fusion.2 = bf16[128,160]{1,0:T(8,128)(2,1)S(1)} fusion(f32[]{:T(128)} %bitcast.102, f32[]{:T(128)} %bitcast.103, f32[]{:T(128)} %bitcast.104, f32[]{:T(128)} %bitcast.105, f32[]{:T(128)} %bitcast.106, f32[]{:T(128)} %bitcast.107, f32[]{:T(128)} %bitcast.108, f32[]{:T(128)} %bitcast.109, f32[]{:T(128)} %bitcast.110, f32[]{:T(128)} %bitcast.111, ...), kind=kLoop, calls=%fused_computation.102 | loop fusion | flops 1351680 | bytes 41084 | tf_op jit(solution)/shard_map/convert_element_type | solution.py:31
  195.7 20.8 %reduce-precision_convert_fusion = bf16[256,256]{1,0:T(8,128)(2,1)S(1)} fusion(f32[]{:T(128)} %bitcast.36, f32[]{:T(128)} %bitcast.37, f32[]{:T(128)} %bitcast.38, f32[]{:T(128)} %bitcast.39, f32[]{:T(128)} %bitcast.40, f32[]{:T(128)} %bitcast.41, f32[]{:T(128)} %bitcast.42, f32[]{:T(128)} %bitcast.43, f32[]{:T(128)} %bitcast.44, f32[]{:T(128)} %bitcast.45, ...), kind=kLoop, calls=%fused_computation.26 | loop fusion | flops 6684672 | bytes 135804 | tf_op jit(solution)/shard_map/convert_element_type | solution.py:31
  216.5 20.8 %fusion.25 = bf16[256,256]{1,0:T(8,128)(2,1)S(1)} fusion(f32[]{:T(128)} %bitcast.36, f32[]{:T(128)} %bitcast.37, f32[]{:T(128)} %bitcast.38, f32[]{:T(128)} %bitcast.39, f32[]{:T(128)} %bitcast.40, f32[]{:T(128)} %bitcast.41, f32[]{:T(128)} %bitcast.42, f32[]{:T(128)} %bitcast.43, f32[]{:T(128)} %bitcast.44, f32[]{:T(128)} %bitcast.45, f32[]{:T(128)} %bitcast.46, ...), kind=kLoop, calls=%fused_computation.30 | loop fusion | flops 6750208 | bytes 135804 | tf_op jit(solution)/shard_map/convert_element_type | solution.py:31
  237.4 20.8 %reduce-precision_convert_fusion.1 = bf16[256,256]{1,0:T(8,128)(2,1)S(1)} fusion(f32[]{:T(128)} %bitcast.66, f32[]{:T(128)} %bitcast.65, f32[]{:T(128)} %bitcast.64, f32[]{:T(128)} %bitcast.63, f32[]{:T(128)} %bitcast.62, f32[]{:T(128)} %bitcast.61, f32[]{:T(128)} %bitcast.60, f32[]{:T(128)} %bitcast.59, f32[]{:T(128)} %bitcast.58, f32[]{:T(128)} %bitcast.57, ...), kind=kLoop, calls=%fused_computation.28 | loop fusion | flops 6684672 | bytes 135804 | tf_op jit(solution)/shard_map/convert_element_type | solution.py:31
  258.2 20.8 %fusion.24 = bf16[256,256]{1,0:T(8,128)(2,1)S(1)} fusion(f32[]{:T(128)} %bitcast.66, f32[]{:T(128)} %bitcast.65, f32[]{:T(128)} %bitcast.64, f32[]{:T(128)} %bitcast.63, f32[]{:T(128)} %bitcast.62, f32[]{:T(128)} %bitcast.61, f32[]{:T(128)} %bitcast.60, f32[]{:T(128)} %bitcast.59, f32[]{:T(128)} %bitcast.58, f32[]{:T(128)} %bitcast.57, f32[]{:T(128)} %bitcast.56, ...), kind=kLoop, calls=%fused_computation.29 | loop fusion | flops 6750208 | bytes 135804 | tf_op jit(solution)/shard_map/convert_element_type | solution.py:31
  279.1 0.7 pad_maximum_fusion.2.rows
  279.9 0.8 pad_maximum_fusion.3.lines
  280.7 0.9 pad_maximum_fusion.1.depth
  281.5 1.3 copy-done
  282.8 73.7 %shard_map.28 = f32[2,2,32,32,128]{4,3,2,1,0:T(8,128)} custom-call(f32[32,128,128]{2,1,0:T(8,128)} %copy-done, bf16[2,512,256]{2,1,0:T(8,128)(2,1)} %pad_maximum_fusion.1.depth, bf16[2,256,256]{2,1,0:T(8,128)(2,1)} %pad_maximum_fusion.2.rows, bf16[2,256,160]{2,1,0:T(8,128)(2,1)} %pad_maximum_fusion.3.lines), custom_call_target="tpu_custom_call" | custom-call | tf_op jit(solution)/shard_map/pallas_call | solution.py:308
  356.5 3.1 copy_bitcast_fusion
  (17 shorter events, 0.4 us)
Async XLA Ops:
  0.0 8.1 %copy-start.1 = (f32[2,1,128,2048]{3,2,1,0:T(8,128)S(1)}, f32[2,1,128,2048]{3,2,1,0:T(8,128)}, u32[]{:S(2)}) copy-start(f32[2,1,128,2048]{3,2,1,0:T(8,128)} %param.2) | copy-start | bytes 6291460
  28.8 7.1 %copy-start.2 = (f32[3,2,31]{2,1,0:T(2,128)S(1)}, f32[3,2,31]{2,1,0:T(2,128)}, u32[]{:S(2)}) copy-start(f32[3,2,31]{2,1,0:T(2,128)} %param.3) | copy-start | bytes 2236
  28.8 252.7 %all-to-all-start = ((f32[32,128,128]{2,1,0:T(8,128)}), f32[32,128,128]{2,1,0:T(8,128)S(1)}, u32[]{:S(2)}, u32[]{:S(2)}) async-start(f32[32,128,128]{2,1,0:T(8,128)} %bitcast.35), calls=%async_computation | async-start | bytes 4194304 | tf_op jit(solution)/shard_map/all_to_all | solution.py:294
  281.5 1.3 copy-start

commit v2 on v1

--- a/solution.py
+++ b/solution.py
@@ -2,6 +2,7 @@
 
 import jax
 import jax.numpy as jnp
+import numpy as np
 from jax import lax
 from jax.experimental import pallas as pl
 from jax.experimental.pallas import tpu as pltpu
@@ -26,39 +27,57 @@
     return kernel_table / jnp.sum(kernel_table, axis=1, keepdims=True)
 
 
-def halves(table):
-    high = lax.reduce_precision(table, 8, 7)
-    return high.astype(jnp.bfloat16), (table - high).astype(jnp.bfloat16)
-
-
-def banded(taps, lag, mask=None):
-    table = jnp.zeros(lag.shape, jnp.float32)
-    for k in range(taps.shape[0]):
-        hit = lag == k
-        table = jnp.where(hit if mask is None else hit & mask, taps[k], table)
-    return table
-
-
-def depth_table(taps, planes):
+def base_row(taps, width, lag_of):
+    place = np.arange(width)
+    lag = lag_of(np.where(place < width // 2, place, place - width))
+    hits = lag[:, None] == np.arange(taps.shape[0])[None, :]
+    return jnp.sum(jnp.where(hits, taps[None, :], 0.0), axis=1)
+
+
+def base_rows(taps, lag_of, reach):
+    width = -(-2 * reach // 128) * 128
+    return jnp.stack([base_row(q, width, lag_of) for q in taps])[:, None, :]
+
+
+def shifted(base, start, count, columns):
+    block = jnp.broadcast_to(base, (count, base.shape[1]))
+    block = pltpu.roll(block, start, 1, stride=1, stride_axis=0)[:, :columns]
+    high = block.astype(jnp.bfloat16)
+    return high, (block - high.astype(jnp.float32)).astype(jnp.bfloat16)
+
+
+def tables_kernel(depth_base, rows_base, lines_base, depth, rows, lines):
+    size, width, cells = depth.shape[2], rows.shape[1] // 2, lines.shape[1] // 2
+    for way in range(2):
+        for start in range(0, size, 256):
+            high, low = shifted(depth_base[way], start, min(256, size), size)
+            depth[way, pl.ds(start, high.shape[0])] = high
+            depth[way, pl.ds(size + start, high.shape[0])] = low
+        high, low = shifted(rows_base[way], 0, width, width)
+        both = jnp.concatenate([high, low], axis=1)
+        rows[way] = jnp.concatenate([both, both], axis=0)
+        high, low = shifted(lines_base[way], 0, cells, lines.shape[2])
+        lines[way] = jnp.concatenate([high, low], axis=0)
+
+
+def filter_tables(taps, planes, width, cells, edge):
+    half = taps.shape[2] // 2
     size = planes * SUB
-    row = lax.broadcasted_iota(jnp.int32, (size, size), 0)
-    col = lax.broadcasted_iota(jnp.int32, (size, size), 1)
-    lag = col // SUB - row // SUB + taps.shape[0] // 2
-    return jnp.concatenate(halves(banded(taps, lag, row % SUB == col % SUB)), axis=0)
-
-
-def rows_table(taps, lines):
-    row = lax.broadcasted_iota(jnp.int32, (lines, lines), 0)
-    col = lax.broadcasted_iota(jnp.int32, (lines, lines), 1)
-    both = jnp.concatenate(halves(banded(taps, row - col + taps.shape[0] // 2)), axis=1)
-    return jnp.concatenate([both, both], axis=0)
-
-
-def lines_table(taps, cells, edge):
-    row = lax.broadcasted_iota(jnp.int32, (cells, cells + 2 * edge), 0)
-    col = lax.broadcasted_iota(jnp.int32, (cells, cells + 2 * edge), 1)
-    lag = col - row - edge + taps.shape[0] // 2
-    return jnp.concatenate(halves(banded(taps, lag)), axis=0)
+    depth = base_rows(taps[:, 0], lambda d: np.where(d % SUB == 0, d // SUB + half, -1), size)
+    rows = base_rows(taps[:, 1], lambda d: half - d, width)
+    lines = base_rows(taps[:, 2], lambda d: d - edge + half, cells + 2 * edge)
+    vmem = pl.BlockSpec(memory_space=pltpu.VMEM)
+    return pl.pallas_call(
+        tables_kernel,
+        out_shape=(
+            jax.ShapeDtypeStruct((2, 2 * size, size), jnp.bfloat16),
+            jax.ShapeDtypeStruct((2, 2 * width, 2 * width), jnp.bfloat16),
+            jax.ShapeDtypeStruct((2, 2 * cells, cells + 2 * edge), jnp.bfloat16),
+        ),
+        in_specs=[vmem] * 3,
+        out_specs=[vmem] * 3,
+        cost_estimate=pl.CostEstimate(flops=1 << 20, bytes_accessed=1 << 22, transcendentals=0),
+    )(depth, rows, lines)
 
 
 def split(value):
@@ -154,23 +173,21 @@
         groups = cells // SUB
         outer = edge // SUB
 
-        for group in range(outer):
-            planes_and_rows(field, slot, way, group)
+        @pl.loop(0, 2 * outer, unroll=2)
+        def _(step):
+            planes_and_rows(field, slot, way, lax.rem(step + groups - outer, groups))
 
         @pl.when(line > 0)
         def _():
             edge_copy(slot, False).start()
 
-        for group in range(groups - outer, groups):
-            planes_and_rows(field, slot, way, group)
-
         @pl.when(line < last)
         def _():
             edge_copy(slot, True).start()
 
         if groups > 2 * outer:
 
-            @pl.loop(outer, groups - outer)
+            @pl.loop(outer, groups - outer, unroll=4 if groups % 4 == 0 else 1)
             def _(group):
                 planes_and_rows(field, slot, way, group)
 
@@ -208,21 +225,21 @@
         source = cleaned if iteration == 0 else estimate
         spread(source, 0, 0)
 
-        @pl.loop(0, planes, unroll=2)
+        @pl.loop(0, planes, unroll=4)
         def _(plane):
             ratio[plane] = cleaned[plane] / (along_lines(0, 0, plane) + BACKGROUND)
 
         spread(ratio, 1, 1)
         if iteration < ITERS - 1:
 
-            @pl.loop(0, planes, unroll=2)
+            @pl.loop(0, planes, unroll=4)
             def _(plane):
                 estimate[plane] = source[plane] * along_lines(1, 1, plane)
 
         else:
             for chunk in range(CHUNKS):
 
-                @pl.loop(chunk * (planes // CHUNKS), (chunk + 1) * (planes // CHUNKS), unroll=2)
+                @pl.loop(chunk * (planes // CHUNKS), (chunk + 1) * (planes // CHUNKS), unroll=4)
                 def _(plane):
                     value = (source[plane] * along_lines(1, 1, plane)).T
                     for target in range(count_gy):
@@ -296,10 +313,8 @@
     channel = lax.axis_index("gx") % channels
     taps = jnp.where(channel == 0, psf_taps[:, 0], psf_taps[:, 1])
     forward = taps / jnp.sum(taps, axis=1, keepdims=True)
-    both = (forward, forward[:, ::-1])
-    depth = jnp.stack([depth_table(q[0], planes) for q in both])
-    rows = jnp.stack([rows_table(q[1], lines_x) for q in both])
-    lines = jnp.stack([lines_table(q[2], cells, edge) for q in both])
+    both = jnp.stack([forward, forward[:, ::-1]])
+    depth, rows, lines = filter_tables(both, planes, lines_x, cells, edge)
 
     per_gx = count_gy // 2
     block_x = lines_x // count_gy

time: 363 us -> 160 us (0.44)
  other arithmetic: 251 us -> 10.3 us
  waiting for transfers between devices: 0.01 us -> 43.5 us
    convert_element_type x12 -> x0, other arithmetic: 239 us -> none  [halves(): return (high.astype(jnp.bfloat16), (table - high).astype(jnp.bfloat16))]
    all_to_all x1, waiting for transfers between devices: 0.01 us -> 43.5 us  [local(): lax.all_to_all(blocks, ('gx', 'gy'), split_axis=0, concat_axis=0, tiled=T...]
    pallas_call x1, Pallas kernels: 73.7 us -> 68.7 us  [local(): pl.pallas_call(functools.partial(deconvolve_kernel, count_gx, count_gy, e...]
  transfers between devices with their start and end apart: 1 -> 1, of which waited for: 0 -> 1; matrix products, arithmetic and copies ran while one was open for 68% -> 2% of each run, Pallas kernels for 0% -> 1%
where the time goes in v2:
time: 160 us; the launch traced here: 159 us
  Pallas kernels  70.7 us (44%)
  waiting for transfers between devices  43.5 us (27%)
  matrix products  15.6 us (10%)
  local copies, waits for them, and re-layouts  12.1 us (8%)
  other arithmetic  10.3 us (6%)
  starting transfers between devices  7.09 us (4%)
    pallas_call x1, Pallas kernels, local(): pl.pallas_call(functools.partial(deconvolve_kernel, count_gx, count_gy, e...  68.7 us
    all_to_all x1, waiting for transfers between devices, local(): lax.all_to_all(blocks, ('gx', 'gy'), split_axis=0, concat_axis=0, tiled=T...  43.5 us
    dot_general x1, matrix products, local(): jnp.einsum('czxj,jy->czxy', smoothed, along_table, precision=lax.Precisio...  14.5 us
    reduce_sum x2, other arithmetic, smoothing_table(): return kernel_table / jnp.sum(kernel_table, axis=1, keepdims=True)  8.12 us
    all_to_all x1, starting transfers between devices, local(): lax.all_to_all(blocks, ('gx', 'gy'), split_axis=0, concat_axis=0, tiled=T...  7.09 us
    reshape x2, local copies, waits for them, and re-layouts, local(): cleaned_plane.reshape(channels, own_planes, lines_x, pairs, count_gy, cells)  5.63 us
  transfers between devices with their start and end apart: 1, of which 1 were waited for; matrix products, arithmetic and copies ran while one was open for 2% of the time, Pallas kernels for 1%

profile of v2, /device:TPU:1, one launch (start us, length us, event | category | flops | bytes accessed | tf_op | source)
XLA Modules:
  0.0 159.4 jit_solution(12519861263788464722)
XLA Ops:
  0.0 0.1 fusion.26
  0.1 0.0 copy-start.1
  0.1 8.0 %fusion.4 = f32[2048]{0:T(1024)S(1)} fusion(), kind=kLoop, calls=%fused_computation.6 | loop fusion | flops 37746688 | bytes 8192 | tf_op jit(solution)/shard_map/reduce_sum | solution.py:27
  8.1 0.0 copy-done.1
  8.2 1.0 fusion.22
  9.2 14.5 %fusion.18 = f32[2,1,128,2048]{3,2,0,1:T(8,128)} fusion(f32[2048]{0:T(1024)S(1)} %fusion.4, f32[128,2,2048]{2,0,1:T(8,128)S(1)} %fusion.22, f32[2,1,128,2048]{3,2,1,0:T(8,128)S(1)} %copy-done.1), kind=kOutput, calls=%fused_computation.14 | convolution fusion | flops 6481772544 | bytes 6299648 | tf_op jit(solution)/shard_map/czxj,jy->czxy/dot_general | solution.py:299
  23.7 3.7 %reshape.75 = f32[2,1,128,4,4,128]{5,4,3,2,0,1:T(4,128)} reshape(f32[2,1,128,2048]{3,2,0,1:T(8,128)} %fusion.18) | data formatting | bytes 4194304 | tf_op jit(solution)/shard_map/reshape | solution.py:304
  27.4 1.9 %copy.27 = f32[2,1,128,4,4,128]{2,5,0,1,4,3:T(8,128)S(1)} copy(f32[2,1,128,4,4,128]{5,4,3,2,0,1:T(4,128)} %reshape.75) | data formatting | bytes 4194304 | tf_op jit(solution)/shard_map/reshape | solution.py:304
  29.4 0.1 slice_bitcast_fusion.15
  29.6 0.1 maximum_bitcast_fusion
  29.7 1.5 pad_maximum_fusion
  31.2 0.0 copy-start.5
  31.2 7.1 %all-to-all-start = ((f32[32,128,128]{2,1,0:T(8,128)}), f32[32,128,128]{2,1,0:T(8,128)S(1)}, u32[]{:S(2)}, u32[]{:S(2)}) async-start(f32[32,128,128]{2,1,0:T(8,128)} %bitcast.35), calls=%async_computation | async-start | bytes 4194304 | tf_op jit(solution)/shard_map/all_to_all | solution.py:311
  38.3 0.0 copy-done.5
  38.3 0.1 fusion.35
  38.4 0.1 bitcast_divide_fusion
  38.5 0.1 rev.3
  38.6 0.1 bitcast_divide_fusion.1
  38.7 0.0 copy-done.3
  38.7 0.1 select_reduce_fusion.3
  38.9 0.6 broadcast_in_dim.99.lines_base
  39.4 0.0 copy-done.2
  39.4 0.1 select_reduce_fusion.1
  39.6 0.6 broadcast_in_dim.87.depth_base
  40.2 0.0 copy-done.4
  40.2 0.1 select_reduce_fusion.5
  40.3 0.6 broadcast_in_dim.93.rows_base
  40.8 2.0 %shard_map.82 = (bf16[2,512,256]{2,1,0:T(8,128)(2,1)}, bf16[2,256,256]{2,1,0:T(8,128)(2,1)}, bf16[2,256,160]{2,1,0:T(8,128)(2,1)}) custom-call(f32[2,1,512]{2,1,0:T(1,128)} %broadcast_in_dim.87.depth_base, f32[2,1,256]{2,1,0:T(1,128)} %broadcast_in_dim.93.rows_base, f32[2,1,384]{2,1,0:T(1,128)} %broadcast_in_dim.99.lines_base), custom_call_target="tpu_custom_call" | custom-call | flops 1048576 | bytes 4194304 | tf_op jit(solution)/shard_map/pallas_call | solution.py:70
  42.8 43.5 %all-to-all-done.cleaned = f32[32,128,128]{2,1,0:T(8,128)S(1)} async-done(((f32[32,128,128]{2,1,0:T(8,128)}), f32[32,128,128]{2,1,0:T(8,128)S(1)}, u32[]{:S(2)}, u32[]{:S(2)}) %all-to-all-start) | async-done | bytes 2097184 | tf_op jit(solution)/shard_map/all_to_all | solution.py:311
  86.3 1.3 copy-done
  87.6 68.7 %shard_map.83 = f32[2,2,32,32,128]{4,3,2,1,0:T(8,128)} custom-call(f32[32,128,128]{2,1,0:T(8,128)} %copy-done, bf16[2,512,256]{2,1,0:T(8,128)(2,1)} %get-tuple-element.8.depth, bf16[2,256,256]{2,1,0:T(8,128)(2,1)} %get-tuple-element.9.rows, bf16[2,256,160]{2,1,0:T(8,128)(2,1)} %get-tuple-element.10.lines), custom_call_target="tpu_custom_call" | custom-call | tf_op jit(solution)/shard_map/pallas_call | solution.py:323
  156.3 3.1 %copy_bitcast_fusion = f32[2,32,32,256]{3,2,1,0:T(8,128)} fusion(f32[2,2,32,32,128]{4,3,2,1,0:T(8,128)} %shard_map.83), kind=kLoop, calls=%fused_computation.15 | loop fusion | bytes 4194304 | tf_op jit(solution)/shard_map/reshape | solution.py:343
  (12 shorter events, 0.1 us)
Async XLA Ops:
  0.1 8.0 %copy-start.1 = (f32[2,1,128,2048]{3,2,1,0:T(8,128)S(1)}, f32[2,1,128,2048]{3,2,1,0:T(8,128)}, u32[]{:S(2)}) copy-start(f32[2,1,128,2048]{3,2,1,0:T(8,128)} %param.8) | copy-start | bytes 6291460
  31.2 7.1 %copy-start.5 = (f32[3,2,31]{2,1,0:T(2,128)S(1)}, f32[3,2,31]{2,1,0:T(2,128)}, u32[]{:S(2)}) copy-start(f32[3,2,31]{2,1,0:T(2,128)} %param.9) | copy-start | bytes 2236
  31.2 7.5 %copy-start.3 = (pred[384,31]{0,1:T(8,128)(4,1)S(1)}, pred[384,31]{0,1:T(8,128)(4,1)}, u32[]{:S(2)}) copy-start(pred[384,31]{0,1:T(8,128)(4,1)} %constant.45.clone) | copy-start | bytes 35716
  31.2 8.2 %copy-start.2 = (pred[512,31]{0,1:T(8,128)(4,1)S(1)}, pred[512,31]{0,1:T(8,128)(4,1)}, u32[]{:S(2)}) copy-start(pred[512,31]{0,1:T(8,128)(4,1)} %constant.43.clone) | copy-start | bytes 47620
  31.2 8.9 %copy-start.4 = (pred[256,31]{0,1:T(8,128)(4,1)S(1)}, pred[256,31]{0,1:T(8,128)(4,1)}, u32[]{:S(2)}) copy-start(pred[256,31]{0,1:T(8,128)(4,1)} %constant.44.clone) | copy-start | bytes 23812
  31.2 55.1 %all-to-all-start = ((f32[32,128,128]{2,1,0:T(8,128)}), f32[32,128,128]{2,1,0:T(8,128)S(1)}, u32[]{:S(2)}, u32[]{:S(2)}) async-start(f32[32,128,128]{2,1,0:T(8,128)} %bitcast.35), calls=%async_computation | async-start | bytes 4194304 | tf_op jit(solution)/shard_map/all_to_all | solution.py:311
  86.3 1.3 copy-start

commit v3 on v2

--- a/solution.py
+++ b/solution.py
@@ -17,14 +17,19 @@
 MESH = pl.DeviceIdType.MESH
 
 
-def smoothing_table(length_cells, spread_cells, circular):
+def smoothing_table(length_cells, spread_cells):
     places = lax.iota(jnp.int32, length_cells)
     offset = jnp.abs(places[:, None] - places[None, :])
-    if circular:
-        offset = jnp.minimum(offset, length_cells - offset)
     scaled = offset.astype(jnp.float32) / spread_cells
     kernel_table = jnp.exp(-0.5 * scaled * scaled)
     return kernel_table / jnp.sum(kernel_table, axis=1, keepdims=True)
+
+
+def circular_row(length_cells, spread_cells):
+    places = lax.broadcasted_iota(jnp.int32, (1, length_cells), 1)
+    scaled = jnp.minimum(places, length_cells - places).astype(jnp.float32) / spread_cells
+    kernel_row = jnp.exp(-0.5 * scaled * scaled)
+    return kernel_row / jnp.sum(kernel_row)
 
 
 def base_row(taps, width, lag_of):
@@ -46,7 +51,7 @@
     return high, (block - high.astype(jnp.float32)).astype(jnp.bfloat16)
 
 
-def tables_kernel(depth_base, rows_base, lines_base, depth, rows, lines):
+def fill_tables(depth_base, rows_base, lines_base, depth, rows, lines):
     size, width, cells = depth.shape[2], rows.shape[1] // 2, lines.shape[1] // 2
     for way in range(2):
         for start in range(0, size, 256):
@@ -60,26 +65,6 @@
         lines[way] = jnp.concatenate([high, low], axis=0)
 
 
-def filter_tables(taps, planes, width, cells, edge):
-    half = taps.shape[2] // 2
-    size = planes * SUB
-    depth = base_rows(taps[:, 0], lambda d: np.where(d % SUB == 0, d // SUB + half, -1), size)
-    rows = base_rows(taps[:, 1], lambda d: half - d, width)
-    lines = base_rows(taps[:, 2], lambda d: d - edge + half, cells + 2 * edge)
-    vmem = pl.BlockSpec(memory_space=pltpu.VMEM)
-    return pl.pallas_call(
-        tables_kernel,
-        out_shape=(
-            jax.ShapeDtypeStruct((2, 2 * size, size), jnp.bfloat16),
-            jax.ShapeDtypeStruct((2, 2 * width, 2 * width), jnp.bfloat16),
-            jax.ShapeDtypeStruct((2, 2 * cells, cells + 2 * edge), jnp.bfloat16),
-        ),
-        in_specs=[vmem] * 3,
-        out_specs=[vmem] * 3,
-        cost_estimate=pl.CostEstimate(flops=1 << 20, bytes_accessed=1 << 22, transcendentals=0),
-    )(depth, rows, lines)
-
-
 def split(value):
     high = value.astype(jnp.bfloat16)
     low = (value - high.astype(jnp.float32)).astype(jnp.bfloat16)
@@ -102,8 +87,9 @@
 
 
 def deconvolve_kernel(
-    count_gx, count_gy, edge, cleaned, depth, rows, lines, out,
-    estimate, ratio, wide, stage, send_sem, recv_sem, out_send, out_recv, own_sem,
+    count_gx, count_gy, edge, raw, across, along_base, depth_base, rows_base, lines_base, out,
+    cleaned, estimate, ratio, wide, stage, along, smooth, depth, rows, lines,
+    held, send_sem, recv_sem, out_send, out_recv, own_sem, plane_send, plane_recv, held_sem,
 ):
     planes, cells, width = cleaned.shape
     size = planes * SUB
@@ -116,6 +102,10 @@
     lines_x = width // count_gy
     me = gx * count_gy + gy
 
+    def load(channel):
+        return pltpu.make_async_copy(raw.at[channel, 0], held, held_sem)
+
+    load(0).start()
     barrier = pltpu.get_barrier_semaphore()
 
     @pl.loop(0, count_gx * count_gy)
@@ -126,7 +116,95 @@
                 barrier, inc=1, device_id=(other // count_gy, other % count_gy), device_id_type=MESH
             )
 
-    pl.semaphore_wait(barrier, count_gx * count_gy - 1)
+    channels, _, _, lines_y = raw.shape
+    block = along.shape[0] // 2
+    blocks = lines_y // block
+    chunks = lines_y // cells
+    per_block = block // cells
+    high, low = shifted(along_base[...], 0, block, lines_y)
+    along[0:block] = high
+    along[block : 2 * block] = low
+
+    def smooth_block(index):
+        columns = pl.ds(pl.multiple_of(index * block, block), block)
+        value = held[:, columns]
+        high = value.astype(jnp.bfloat16)
+        low = (value - high.astype(jnp.float32)).astype(jnp.bfloat16)
+        product = jnp.dot(across[...], high, preferred_element_type=jnp.float32)
+        total = product[:width] + product[width:]
+        total += jnp.dot(across[0:width], low, preferred_element_type=jnp.float32)
+        high = total.astype(jnp.bfloat16)
+        smooth[0:width, columns] = high
+        smooth[width : 2 * width, columns] = (total - high.astype(jnp.float32)).astype(jnp.bfloat16)
+
+    def clean_block(channel, index):
+        total = jnp.zeros((width, block), jnp.float32)
+        for other in range(blocks):
+            columns = pl.ds(other * block, block)
+            shift = lax.rem(index - other + blocks, blocks)
+            table = pl.ds(pl.multiple_of(shift * block, block), block)
+            product = jnp.dot(
+                smooth[:, columns], along[0:block, table], preferred_element_type=jnp.float32
+            )
+            total += product[:width] + product[width:]
+            total += jnp.dot(
+                smooth[0:width, columns], along[block : 2 * block, table],
+                preferred_element_type=jnp.float32,
+            )
+        columns = pl.ds(pl.multiple_of(index * block, block), block)
+        smoothed = smooth[0:width, columns].astype(jnp.float32)
+        smoothed += smooth[width : 2 * width, columns].astype(jnp.float32)
+        value = jnp.maximum(held[:, columns] - (smoothed - total), 0.0)
+        estimate[pl.ds(channel * chunks + index * per_block, per_block)] = value.T.reshape(
+            per_block, cells, width
+        )
+
+    def plane_copy(channel, chunk):
+        target_pair, target_gy = device_of(count_gy, chunk)
+        return pltpu.make_async_remote_copy(
+            src_ref=estimate.at[channel * chunks + chunk],
+            dst_ref=cleaned.at[me],
+            send_sem=plane_send.at[channel * chunks + chunk],
+            recv_sem=plane_recv.at[me],
+            device_id=(target_pair * 2 + channel, target_gy),
+            device_id_type=MESH,
+        )
+
+    own_plane = pltpu.make_async_copy(
+        estimate.at[core * chunks + line], cleaned.at[me], plane_send.at[core * chunks + line]
+    )
+
+    def is_own_plane(channel, chunk):
+        return jnp.logical_and(channel == core, chunk == line)
+
+    for channel in range(channels):
+        if channel > 0:
+            load(channel).start()
+        load(channel).wait()
+
+        @pl.loop(0, blocks, unroll=2)
+        def _(index):
+            smooth_block(index)
+
+        if channel == 0:
+            pl.semaphore_wait(barrier, count_gx * count_gy - 1)
+
+        @pl.loop(0, blocks)
+        def _(step):
+            index = lax.rem(step + (line + 1) // per_block + blocks // 2, blocks)
+            clean_block(channel, index)
+            for part in range(per_block):
+                chunk = index * per_block + part
+
+                @pl.when(is_own_plane(channel, chunk))
+                def _():
+                    own_plane.start()
+
+                @pl.when(jnp.logical_not(is_own_plane(channel, chunk)))
+                def _():
+                    plane_copy(channel, chunk).start()
+
+    fill_tables(depth_base, rows_base, lines_base, depth, rows, lines)
 
     zeros = jnp.zeros((planes, edge, width), jnp.float32)
 
@@ -139,6 +217,28 @@
     def _():
         for slot in range(2):
             wide[slot, :, edge + cells :, :] = zeros
+
+    own_plane.wait()
+    for channel in range(channels):
+
+        @pl.loop(0, chunks)
+        def _(chunk):
+            @pl.when(jnp.logical_not(is_own_plane(channel, chunk)))
+            def _():
+                plane_copy(channel, chunk).wait_send()
+
+    @pl.loop(0, count_gx * count_gy)
+    def _(other):
+        @pl.when(other != me)
+        def _():
+            pltpu.make_async_remote_copy(
+                src_ref=estimate.at[0],
+                dst_ref=cleaned.at[other],
+                send_sem=plane_send.at[0],
+                recv_sem=plane_recv.at[other],
+                device_id=(gx, gy),
+                device_id_type=MESH,
+            ).wait_recv()
 
     def edge_copy(slot, up):
         target_pair, target_gy = device_of(count_gy, line + (1 if up else -1))
@@ -293,28 +393,22 @@
     planes = own_planes * count_gx * count_gy
     edge = -(-half_taps // SUB) * SUB
 
-    across_table = smoothing_table(lines_x, SIGMA_ACROSS, False)
-    along_table = smoothing_table(lines_y, SIGMA_ALONG, True)
-    smoothed = jnp.einsum("ij,czjy->cziy", across_table, raw_stack, precision=lax.Precision.HIGH)
-    stripes = smoothed - jnp.einsum(
-        "czxj,jy->czxy", smoothed, along_table, precision=lax.Precision.HIGH
-    )
-    cleaned_plane = jnp.maximum(raw_stack - stripes, 0.0)
-
-    blocks = cleaned_plane.reshape(channels, own_planes, lines_x, pairs, count_gy, cells)
-    blocks = jnp.transpose(blocks, (3, 0, 4, 1, 5, 2))
-    ordered = []
-    for pair in range(pairs):
-        order = [place_of(count_gy, pair, gy) for gy in range(count_gy)]
-        ordered.append(jnp.stack([blocks[pair, :, place] for place in order], axis=1))
-    blocks = jnp.stack(ordered).reshape(count_gx * count_gy * own_planes, cells, lines_x)
-    cleaned = lax.all_to_all(blocks, ("gx", "gy"), split_axis=0, concat_axis=0, tiled=True)
+    across_table = smoothing_table(lines_x, SIGMA_ACROSS)
+    high = lax.reduce_precision(across_table, 8, 7)
+    across = jnp.concatenate([high, across_table - high], axis=0).astype(jnp.bfloat16)
+    along_base = circular_row(lines_y, SIGMA_ALONG)
+    block = min(lines_y, 256)
 
     channel = lax.axis_index("gx") % channels
     taps = jnp.where(channel == 0, psf_taps[:, 0], psf_taps[:, 1])
     forward = taps / jnp.sum(taps, axis=1, keepdims=True)
     both = jnp.stack([forward, forward[:, ::-1]])
-    depth, rows, lines = filter_tables(both, planes, lines_x, cells, edge)
+    size = planes * SUB
+    depth = base_rows(
+        both[:, 0], lambda d: np.where(d % SUB == 0, d // SUB + half_taps, -1), size
+    )
+    rows = base_rows(both[:, 1], lambda d: half_taps - d, lines_x)
+    lines = base_rows(both[:, 2], lambda d: d - edge + half_taps, cells + 2 * edge)
 
     per_gx = count_gy // 2
     block_x = lines_x // count_gy
@@ -323,23 +417,33 @@
     gathered = pl.pallas_call(
         functools.partial(deconvolve_kernel, count_gx, count_gy, edge),
         out_shape=jax.ShapeDtypeStruct((channels, per_gx, planes, block_x, cells), jnp.float32),
-        in_specs=[vmem] * 4,
+        in_specs=[pl.BlockSpec(memory_space=pl.ANY)] + [vmem] * 5,
         out_specs=pl.BlockSpec(memory_space=pl.ANY),
         scratch_shapes=[
             field,
             field,
+            field,
             pltpu.VMEM((2, planes, cells + 2 * edge, lines_x), jnp.float32),
             pltpu.VMEM((count_gy, planes, block_x, cells), jnp.float32),
+            pltpu.VMEM((2 * block, lines_y), jnp.bfloat16),
+            pltpu.VMEM((2 * lines_x, lines_y), jnp.bfloat16),
+            pltpu.VMEM((2, 2 * size, size), jnp.bfloat16),
+            pltpu.VMEM((2, 2 * lines_x, 2 * lines_x), jnp.bfloat16),
+            pltpu.VMEM((2, 2 * cells, cells + 2 * edge), jnp.bfloat16),
+            pltpu.VMEM((lines_x, lines_y), jnp.float32),
             pltpu.SemaphoreType.DMA((2, 2)),
             pltpu.SemaphoreType.DMA((2, 2)),
             pltpu.SemaphoreType.DMA((CHUNKS, count_gy)),
             pltpu.SemaphoreType.DMA((CHUNKS, channels, per_gx)),
             pltpu.SemaphoreType.DMA((CHUNKS,)),
+            pltpu.SemaphoreType.DMA((planes,)),
+            pltpu.SemaphoreType.DMA((planes,)),
+            pltpu.SemaphoreType.DMA,
         ],
         compiler_params=pltpu.CompilerParams(
-            collective_id=0, has_side_effects=True, vmem_limit_bytes=60 * 1024 * 1024
+            collective_id=0, has_side_effects=True, vmem_limit_bytes=67043328
         ),
-    )(cleaned, depth, rows, lines)
+    )(raw_stack, across, along_base, depth, rows, lines)
     return jnp.transpose(gathered, (0, 2, 3, 1, 4)).reshape(
         channels, planes, block_x, per_gx * cells
     )

time: 160 us -> 132 us (0.82)
  Pallas kernels: 70.7 us -> 120 us
  waiting for transfers between devices: 43.5 us -> 0 us
  matrix products: 15.6 us -> 0 us
  local copies, waits for them, and re-layouts: 12.1 us -> 5 us
  starting transfers between devices: 7.09 us -> 0 us
  other arithmetic: 10.3 us -> 6.21 us
    pallas_call x1, Pallas kernels: 68.7 us -> 120 us  [local(): pl.pallas_call(functools.partial(deconvolve_kernel, count_gx, count_gy, e...]
    all_to_all x1 -> x0, waiting for transfers between devices: 43.5 us -> none  [local(): lax.all_to_all(blocks, ('gx', 'gy'), split_axis=0, concat_axis=0, tiled=T...]
    dot_general x2 -> x0, matrix products: 15.6 us -> none  [the longest x1 14.5 us: local(): jnp.einsum('czxj,jy->czxy', smoothed, along_table, precision=lax.Precisio...]
    reduce_sum x2 -> x1, other arithmetic: 8.12 us -> 0.12 us  [smoothing_table(): return kernel_table / jnp.sum(kernel_table, axis=1, keepdims=True)]
    all_to_all x1 -> x0, starting transfers between devices: 7.09 us -> none  [local(): lax.all_to_all(blocks, ('gx', 'gy'), split_axis=0, concat_axis=0, tiled=T...]
    reshape x2 -> x0, local copies, waits for them, and re-layouts: 5.63 us -> none  [local(): cleaned_plane.reshape(channels, own_planes, lines_x, pairs, count_gy, cells)]
    reduce_sum x3, other arithmetic: 0.28 us -> 2.4 us  [base_row(): return jnp.sum(jnp.where(hits, taps[None, :], 0.0), axis=1)]
    pallas_call x1 -> x0, Pallas kernels: 1.96 us -> none  [filter_tables(): pl.pallas_call(tables_kernel, out_shape=(jax.ShapeDtypeStruct((2, 2 * siz...]
  transfers between devices with their start and end apart: 1 -> 0, of which waited for: 1 -> 0; matrix products, arithmetic and copies ran while one was open for 2% -> 0% of each run, Pallas kernels for 1% -> 0%
where the time goes in v3:
time: 132 us
  Pallas kernels  120 us (91%)
  other arithmetic  6.21 us (5%)
  local copies, waits for them, and re-layouts  5 us (4%)
    pallas_call x1, Pallas kernels, local(): pl.pallas_call(functools.partial(deconvolve_kernel, count_gx, count_gy, e...  120 us
    reshape x1, local copies, waits for them, and re-layouts, local(): jnp.transpose(gathered, (0, 2, 3, 1, 4))  3.1 us

profile of v3, /device:TPU:1, one launch (start us, length us, event | category | flops | bytes accessed | tf_op | source)
XLA Modules:
  0.0 131.6 jit_solution(11132690850971649727)
XLA Ops:
  0.0 0.6 fusion.4
  0.6 0.1 fusion.2
  0.8 0.9 fusion.5
  1.6 0.1 bitcast_divide_fusion.1
  1.7 0.1 bitcast_divide_fusion
  1.8 0.1 rev.3
  1.9 0.8 select_reduce_fusion.5
  2.7 0.6 broadcast_in_dim.90.rows_base
  3.3 0.8 select_reduce_fusion.3
  4.1 0.6 broadcast_in_dim.96.lines_base
  4.7 0.8 select_reduce_fusion.1
  5.6 0.6 broadcast_in_dim.84.depth_base
  6.1 1.3 broadcast_divide_fusion.along_base
  7.4 0.1 reduce-precision_convert_fusion
  7.5 0.6 pad_maximum_fusion.across
  8.2 120.4 %shard_map.82 = f32[2,2,32,32,128]{4,3,2,1,0:T(8,128)} custom-call(f32[2,1,128,2048]{3,2,1,0:T(8,128)} %raw.1, bf16[256,128]{1,0:T(8,128)(2,1)} %pad_maximum_fusion.across, f32[1,2048]{1,0:T(1,128)} %broadcast_divide_fusion.along_base, f32[2,1,512]{2,1,0:T(1,128)} %broadcast_in_dim.84.depth_base, f32[2,1,256]{2,1,0:T(1,128)} %broadcast_in_dim.90.rows_base, ...), custom_call_target="tpu_custom_call" | custom-call | tf_op jit(solution)/shard_map/pallas_call | solution.py:417
  128.5 3.1 %copy_bitcast_fusion = f32[2,32,32,256]{3,2,1,0:T(8,128)} fusion(f32[2,2,32,32,128]{4,3,2,1,0:T(8,128)} %shard_map.82), kind=kLoop, calls=%fused_computation | loop fusion | bytes 4194304 | tf_op jit(solution)/shard_map/reshape | solution.py:447
  (7 shorter events, 0.0 us)

commit v4 on v3

--- a/solution.py
+++ b/solution.py
@@ -2,7 +2,6 @@
 
 import jax
 import jax.numpy as jnp
-import numpy as np
 from jax import lax
 from jax.experimental import pallas as pl
 from jax.experimental.pallas import tpu as pltpu
@@ -18,9 +17,9 @@
 
 
 def smoothing_table(length_cells, spread_cells):
-    places = lax.iota(jnp.int32, length_cells)
-    offset = jnp.abs(places[:, None] - places[None, :])
-    scaled = offset.astype(jnp.float32) / spread_cells
+    rows = lax.broadcasted_iota(jnp.int32, (length_cells, length_cells), 0)
+    columns = lax.broadcasted_iota(jnp.int32, (length_cells, length_cells), 1)
+    scaled = (rows - columns).astype(jnp.float32) / spread_cells
     kernel_table = jnp.exp(-0.5 * scaled * scaled)
     return kernel_table / jnp.sum(kernel_table, axis=1, keepdims=True)
 
@@ -29,19 +28,23 @@
     places = lax.broadcasted_iota(jnp.int32, (1, length_cells), 1)
     scaled = jnp.minimum(places, length_cells - places).astype(jnp.float32) / spread_cells
     kernel_row = jnp.exp(-0.5 * scaled * scaled)
-    return kernel_row / jnp.sum(kernel_row)
-
-
-def base_row(taps, width, lag_of):
-    place = np.arange(width)
-    lag = lag_of(np.where(place < width // 2, place, place - width))
-    hits = lag[:, None] == np.arange(taps.shape[0])[None, :]
-    return jnp.sum(jnp.where(hits, taps[None, :], 0.0), axis=1)
-
-
-def base_rows(taps, lag_of, reach):
+    return kernel_row / jnp.sum(kernel_row, axis=1, keepdims=True)
+
+
+def base_rows(taps, axis, channel, reach, lag_of):
+    count = taps.shape[2]
     width = -(-2 * reach // 128) * 128
-    return jnp.stack([base_row(q, width, lag_of) for q in taps])[:, None, :]
+    place = lax.broadcasted_iota(jnp.int32, (1, width), 1)
+    lag = lag_of(jnp.where(place < width // 2, place, place - width))
+    forward = jnp.zeros((1, width), jnp.float32)
+    backward = forward
+    total = forward
+    for k in range(count):
+        tap = taps[axis, channel, k]
+        total = total + tap
+        forward = jnp.where(lag == k, tap, forward)
+        backward = jnp.where(lag == count - 1 - k, tap, backward)
+    return forward / total, backward / total
 
 
 def shifted(base, start, count, columns):
@@ -51,8 +54,15 @@
     return high, (block - high.astype(jnp.float32)).astype(jnp.bfloat16)
 
 
-def fill_tables(depth_base, rows_base, lines_base, depth, rows, lines):
-    size, width, cells = depth.shape[2], rows.shape[1] // 2, lines.shape[1] // 2
+def fill_tables(taps, channel, edge, cells, depth, rows, middle, ends):
+    size, width = depth.shape[2], rows.shape[1] // 2
+    half = taps.shape[2] // 2
+    depth_base = base_rows(
+        taps, 0, channel, size,
+        lambda d: jnp.where((d & (SUB - 1)) == 0, (d >> (SUB.bit_length() - 1)) + half, -1),
+    )
+    rows_base = base_rows(taps, 1, channel, width, lambda d: half - d)
+    lines_base = base_rows(taps, 2, channel, max(cells, 3 * edge), lambda d: d - edge + half)
     for way in range(2):
         for start in range(0, size, 256):
             high, low = shifted(depth_base[way], start, min(256, size), size)
@@ -61,8 +71,11 @@
         high, low = shifted(rows_base[way], 0, width, width)
         both = jnp.concatenate([high, low], axis=1)
         rows[way] = jnp.concatenate([both, both], axis=0)
-        high, low = shifted(lines_base[way], 0, cells, lines.shape[2])
-        lines[way] = jnp.concatenate([high, low], axis=0)
+        if cells > 2 * edge:
+            high, low = shifted(lines_base[way], 0, cells - 2 * edge, cells)
+            middle[way] = jnp.concatenate([high, low], axis=0)
+        high, low = shifted(lines_base[way], 0, edge, 3 * edge)
+        ends[way] = jnp.concatenate([high, low], axis=0)
 
 
 def split(value):
@@ -87,8 +100,8 @@
 
 
 def deconvolve_kernel(
-    count_gx, count_gy, edge, raw, across, along_base, depth_base, rows_base, lines_base, out,
-    cleaned, estimate, ratio, wide, stage, along, smooth, depth, rows, lines,
+    count_gx, count_gy, edge, raw, taps, out,
+    cleaned, estimate, ratio, wide, stage, along, smooth, across, depth, rows, middle, ends,
     held, send_sem, recv_sem, out_send, out_recv, own_sem, plane_send, plane_recv, held_sem,
 ):
     planes, cells, width = cleaned.shape
@@ -121,7 +134,11 @@
     blocks = lines_y // block
     chunks = lines_y // cells
     per_block = block // cells
-    high, low = shifted(along_base[...], 0, block, lines_y)
+    table = smoothing_table(width, SIGMA_ACROSS)
+    high = table.astype(jnp.bfloat16)
+    across[0:width] = high
+    across[width : 2 * width] = (table - high.astype(jnp.float32)).astype(jnp.bfloat16)
+    high, low = shifted(circular_row(lines_y, SIGMA_ALONG), 0, block, lines_y)
     along[0:block] = high
     along[block : 2 * block] = low
 
@@ -204,7 +221,7 @@
                 def _():
                     plane_copy(channel, chunk).start()
 
-    fill_tables(depth_base, rows_base, lines_base, depth, rows, lines)
+    fill_tables(taps, core, edge, cells, depth, rows, middle, ends)
 
     zeros = jnp.zeros((planes, edge, width), jnp.float32)
 
@@ -264,16 +281,29 @@
         value = value[:, :width] + value[:, width:]
         wide[slot, :, pl.ds(edge + start, SUB), :] = value.reshape(planes, SUB, width)
 
-    def along_lines(slot, way, plane):
-        value = jnp.dot(lines[way], split(wide[slot, plane]), preferred_element_type=jnp.float32)
-        value = value[:cells] + value[cells:]
+    inner = cells - 2 * edge
+
+    def along_middle(slot, way, plane):
+        value = split(wide[slot, plane, edge : edge + cells])
+        value = jnp.dot(middle[way], value, preferred_element_type=jnp.float32)
+        value = value[:inner] + value[inner:]
         return value[:, :width] + value[:, width:]
 
-    def spread(field, slot, way):
-        groups = cells // SUB
-        outer = edge // SUB
-
-        @pl.loop(0, 2 * outer, unroll=2)
+    def along_ends(slot, way, plane):
+        low = wide[slot, plane, 0 : 3 * edge]
+        high = wide[slot, plane, cells - edge : cells + 2 * edge]
+        value = split(jnp.concatenate([low, high], axis=1))
+        value = jnp.dot(ends[way], value, preferred_element_type=jnp.float32)
+        value = value[:edge] + value[edge:]
+        value = value[:, : 2 * width] + value[:, 2 * width :]
+        return value[:, :width], value[:, width:]
+
+    unroll = 4 if size <= 256 else 1
+    groups = cells // SUB
+    outer = edge // SUB
+
+    def filter_ends(field, slot, way):
+        @pl.loop(0, 2 * outer, unroll=4 if size <= 256 else 1)
         def _(step):
             planes_and_rows(field, slot, way, lax.rem(step + groups - outer, groups))
 
@@ -285,12 +315,14 @@
         def _():
             edge_copy(slot, True).start()
 
-        if groups > 2 * outer:
-
-            @pl.loop(outer, groups - outer, unroll=4 if groups % 4 == 0 else 1)
+    def filter_middle(field, slot, way):
+        if inner:
+
+            @pl.loop(outer, groups - outer, unroll=4 if size <= 256 and groups % 4 == 0 else 1)
             def _(group):
                 planes_and_rows(field, slot, way, group)
 
+    def wait_ends(slot):
         @pl.when(line > 0)
         def _():
             edge_copy(slot, False).wait_send()
@@ -321,27 +353,57 @@
     def is_own(target_gy):
         return jnp.logical_and(target_gy == gy, place // per_gx == core)
 
+    low_end = slice(0, edge)
+    high_end = slice(cells - edge, cells)
+    between = slice(edge, cells - edge)
+    filter_ends(cleaned, 0, 0)
     for iteration in range(ITERS):
         source = cleaned if iteration == 0 else estimate
-        spread(source, 0, 0)
-
-        @pl.loop(0, planes, unroll=4)
+        filter_middle(source, 0, 0)
+        if inner:
+
+            @pl.loop(0, planes, unroll=unroll)
+            def _(plane):
+                blurred = along_middle(0, 0, plane) + BACKGROUND
+                ratio[plane, between] = cleaned[plane, between] / blurred
+
+        wait_ends(0)
+
+        @pl.loop(0, planes, unroll=unroll)
         def _(plane):
-            ratio[plane] = cleaned[plane] / (along_lines(0, 0, plane) + BACKGROUND)
-
-        spread(ratio, 1, 1)
+            low, high = along_ends(0, 0, plane)
+            ratio[plane, low_end] = cleaned[plane, low_end] / (low + BACKGROUND)
+            ratio[plane, high_end] = cleaned[plane, high_end] / (high + BACKGROUND)
+
+        filter_ends(ratio, 1, 1)
+        filter_middle(ratio, 1, 1)
+        if inner:
+
+            @pl.loop(0, planes, unroll=unroll)
+            def _(plane):
+                estimate[plane, between] = source[plane, between] * along_middle(1, 1, plane)
+
+        wait_ends(1)
         if iteration < ITERS - 1:
 
-            @pl.loop(0, planes, unroll=4)
+            @pl.loop(0, planes, unroll=unroll)
             def _(plane):
-                estimate[plane] = source[plane] * along_lines(1, 1, plane)
-
+                low, high = along_ends(1, 1, plane)
+                estimate[plane, low_end] = source[plane, low_end] * low
+                estimate[plane, high_end] = source[plane, high_end] * high
+
+            filter_ends(estimate, 0, 0)
         else:
             for chunk in range(CHUNKS):
 
-                @pl.loop(chunk * (planes // CHUNKS), (chunk + 1) * (planes // CHUNKS), unroll=4)
+                @pl.loop(chunk * (planes // CHUNKS), (chunk + 1) * (planes // CHUNKS), unroll=unroll)
                 def _(plane):
-                    value = (source[plane] * along_lines(1, 1, plane)).T
+                    low, high = along_ends(1, 1, plane)
+                    pieces = [source[plane, low_end] * low]
+                    if inner:
+                        pieces.append(estimate[plane, between])
+                    pieces.append(source[plane, high_end] * high)
+                    value = jnp.concatenate(pieces, axis=0).T
                     for target in range(count_gy):
                         stage[target, plane] = value[target * lines_x : (target + 1) * lines_x]
 
@@ -393,31 +455,15 @@
     planes = own_planes * count_gx * count_gy
     edge = -(-half_taps // SUB) * SUB
 
-    across_table = smoothing_table(lines_x, SIGMA_ACROSS)
-    high = lax.reduce_precision(across_table, 8, 7)
-    across = jnp.concatenate([high, across_table - high], axis=0).astype(jnp.bfloat16)
-    along_base = circular_row(lines_y, SIGMA_ALONG)
     block = min(lines_y, 256)
-
-    channel = lax.axis_index("gx") % channels
-    taps = jnp.where(channel == 0, psf_taps[:, 0], psf_taps[:, 1])
-    forward = taps / jnp.sum(taps, axis=1, keepdims=True)
-    both = jnp.stack([forward, forward[:, ::-1]])
     size = planes * SUB
-    depth = base_rows(
-        both[:, 0], lambda d: np.where(d % SUB == 0, d // SUB + half_taps, -1), size
-    )
-    rows = base_rows(both[:, 1], lambda d: half_taps - d, lines_x)
-    lines = base_rows(both[:, 2], lambda d: d - edge + half_taps, cells + 2 * edge)
-
     per_gx = count_gy // 2
     block_x = lines_x // count_gy
     field = pltpu.VMEM((planes, cells, lines_x), jnp.float32)
-    vmem = pl.BlockSpec(memory_space=pltpu.VMEM)
     gathered = pl.pallas_call(
         functools.partial(deconvolve_kernel, count_gx, count_gy, edge),
         out_shape=jax.ShapeDtypeStruct((channels, per_gx, planes, block_x, cells), jnp.float32),
-        in_specs=[pl.BlockSpec(memory_space=pl.ANY)] + [vmem] * 5,
+        in_specs=[pl.BlockSpec(memory_space=pl.ANY), pl.BlockSpec(memory_space=pltpu.SMEM)],
         out_specs=pl.BlockSpec(memory_space=pl.ANY),
         scratch_shapes=[
             field,
@@ -427,9 +473,11 @@
             pltpu.VMEM((count_gy, planes, block_x, cells), jnp.float32),
             pltpu.VMEM((2 * block, lines_y), jnp.bfloat16),
             pltpu.VMEM((2 * lines_x, lines_y), jnp.bfloat16),
+            pltpu.VMEM((2 * lines_x, lines_x), jnp.bfloat16),
             pltpu.VMEM((2, 2 * size, size), jnp.bfloat16),
             pltpu.VMEM((2, 2 * lines_x, 2 * lines_x), jnp.bfloat16),
-            pltpu.VMEM((2, 2 * cells, cells + 2 * edge), jnp.bfloat16),
+            pltpu.VMEM((2, 2 * max(cells - 2 * edge, edge), cells), jnp.bfloat16),
+            pltpu.VMEM((2, 2 * edge, 3 * edge), jnp.bfloat16),
             pltpu.VMEM((lines_x, lines_y), jnp.float32),
             pltpu.SemaphoreType.DMA((2, 2)),
             pltpu.SemaphoreType.DMA((2, 2)),
@@ -443,7 +491,7 @@
         compiler_params=pltpu.CompilerParams(
             collective_id=0, has_side_effects=True, vmem_limit_bytes=67043328
         ),
-    )(raw_stack, across, along_base, depth, rows, lines)
+    )(raw_stack, psf_taps)
     return jnp.transpose(gathered, (0, 2, 3, 1, 4)).reshape(
         channels, planes, block_x, per_gx * cells
     )

time: 132 us -> 120 us (0.909)
  other arithmetic: 6.21 us -> 0 us
  Pallas kernels: 120 us -> 117 us
  local copies, waits for them, and re-layouts: 5 us -> 3.1 us
    reduce_sum x6 -> x0, other arithmetic: 4.03 us -> none  [the longest x3 2.4 us: base_row(): return jnp.sum(jnp.where(hits, taps[None, :], 0.0), axis=1)]
    pallas_call x1, Pallas kernels: 120 us -> 117 us  [local(): pl.pallas_call(functools.partial(deconvolve_kernel, count_gx, count_gy, e...]
    broadcast_in_dim x5 -> x0, local copies, waits for them, and re-layouts: 1.8 us -> none  [the longest x3 1.79 us: base_rows(): return jnp.stack([base_row(q, width, lag_of) for q in taps])[:, None, :]]
    div x3 -> x0, other arithmetic: 1.42 us -> none  [the longest x1 1.27 us: circular_row(): return kernel_row / jnp.sum(kernel_row)]
where the time goes in v4:
time: 120 us
  Pallas kernels  117 us (98%)
  local copies, waits for them, and re-layouts  3.1 us (3%)
    pallas_call x1, Pallas kernels, local(): pl.pallas_call(functools.partial(deconvolve_kernel, count_gx, count_gy, e...  117 us
    reshape x1, local copies, waits for them, and re-layouts, local(): jnp.transpose(gathered, (0, 2, 3, 1, 4))  3.1 us

profile of v4, /device:TPU:1, one launch (start us, length us, event | category | flops | bytes accessed | tf_op | source)
XLA Modules:
  0.0 120.0 jit_solution(12773579103872353338)
XLA Ops:
  0.0 116.9 %shard_map.28 = f32[2,2,32,32,128]{4,3,2,1,0:T(8,128)} custom-call(f32[2,1,128,2048]{3,2,1,0:T(8,128)} %raw.1, f32[3,2,31]{2,1,0:T(2,128)} %taps.1), custom_call_target="tpu_custom_call" | custom-call | tf_op jit(solution)/shard_map/pallas_call | solution.py:463
  116.9 3.1 %copy_bitcast_fusion = f32[2,32,32,256]{3,2,1,0:T(8,128)} fusion(f32[2,2,32,32,128]{4,3,2,1,0:T(8,128)} %shard_map.28), kind=kLoop, calls=%fused_computation | loop fusion | bytes 4194304 | tf_op jit(solution)/shard_map/reshape | solution.py:495

commit v5 on v4

--- a/solution.py
+++ b/solution.py
@@ -298,7 +298,7 @@
         value = value[:, : 2 * width] + value[:, 2 * width :]
         return value[:, :width], value[:, width:]
 
-    unroll = 4 if size <= 256 else 1
+    unroll = 8 if size <= 256 else 1
     groups = cells // SUB
     outer = edge // SUB
 
@@ -407,7 +407,8 @@
                     for target in range(count_gy):
                         stage[target, plane] = value[target * lines_x : (target + 1) * lines_x]
 
-                for target in range(count_gy):
+                for step in range(count_gy):
+                    target = lax.rem(gy + 1 + step, count_gy)
 
                     @pl.when(is_own(target))
                     def _():

time: 120 us -> 118 us (0.983)
  Pallas kernels: 117 us -> 114 us
    pallas_call x1, Pallas kernels: 117 us -> 114 us  [local(): pl.pallas_call(functools.partial(deconvolve_kernel, count_gx, count_gy, e...]
where the time goes in v5:
time: 118 us; the launch traced here: 117 us
  Pallas kernels  114 us (97%)
  local copies, waits for them, and re-layouts  3.1 us (3%)
    pallas_call x1, Pallas kernels, local(): pl.pallas_call(functools.partial(deconvolve_kernel, count_gx, count_gy, e...  114 us
    reshape x1, local copies, waits for them, and re-layouts, local(): jnp.transpose(gathered, (0, 2, 3, 1, 4))  3.1 us

profile of v5, /device:TPU:1, one launch (start us, length us, event | category | flops | bytes accessed | tf_op | source)
XLA Modules:
  0.0 117.2 jit_solution(17478814978637800478)
XLA Ops:
  0.0 114.0 %shard_map.28 = f32[2,2,32,32,128]{4,3,2,1,0:T(8,128)} custom-call(f32[2,1,128,2048]{3,2,1,0:T(8,128)} %raw.1, f32[3,2,31]{2,1,0:T(2,128)} %taps.1), custom_call_target="tpu_custom_call" | custom-call | tf_op jit(solution)/shard_map/pallas_call | solution.py:464
  114.1 3.1 %copy_bitcast_fusion = f32[2,32,32,256]{3,2,1,0:T(8,128)} fusion(f32[2,2,32,32,128]{4,3,2,1,0:T(8,128)} %shard_map.28), kind=kLoop, calls=%fused_computation | loop fusion | bytes 4194304 | tf_op jit(solution)/shard_map/reshape | solution.py:496
